TPU v7x, 32 devices: a whole 2x2x4 slice. The times are simulated.
32 devices in a mesh: section: 4 (over y, core), expert: 8 (over z, x).
Axes of the slice: x: 2, y: 2, z: 4, core: 2. Of those that a mesh axis runs over, the one named last changes fastest.
Arguments:
- activations: bfloat16 [2048, 6144], P('expert', 'section'), may hold values from -6 to 6
- router_weight: bfloat16 [8, 6144], P(None, 'section'), may hold values from -0.078125 to 0.078125
- w_up: bfloat16 [65536, 6144], P('expert', 'section'), may hold values from -0.078125 to 0.078125
- w_down: bfloat16 [65536, 6144], P('expert', 'section'), may hold values from -0.0625 to 0.0625
- expert_ids: int32 [2048, 2], P('expert'), may hold values from 0 to 7, all different within a row; in each aligned block of 256 rows (0 to 255, 256 to 511, ...) at most 64 rows name the same one
Outputs:
- layer_out: bfloat16 [2048, 6144], P('expert', 'section')
Inputs may be any that keep to these rules, and one draw needn't show every extreme that they name: `expert_ids`: among the 256 tokens of one device (one aligned block of rows) each expert is named exactly 64 times; the two ids of a token differ.
All inputs are finite; a program needn't handle non-finite values.
Results may differ from a plain program's by a relative error of at most 0.009.
Values may be sent and summed in bfloat16 or wider, within the bound.
No kernel may reach another device: no remote copies, remote signals or barrier semaphores. Data moves between devices by JAX's collectives and lax.ppermute only.
A program may use at most 192 MiB of HBM per device.

v0:
```python
import jax
import jax.numpy as jnp
from jax import lax
from jax.sharding import PartitionSpec as P


def body(activations, router_weight, w_up, w_down, expert_ids):
    group = lax.axis_size("expert")
    experts = router_weight.shape[0]
    quarters = group // experts
    tok_rows = activations.shape[0]
    columns = activations.shape[1]
    capacity = tok_rows // 4
    total_rows = experts * capacity
    partial_logits = lax.dot_general(
        activations, router_weight, (((1,), (1,)), ((), ())), preferred_element_type=jnp.float32
    )
    logits = lax.psum(partial_logits, "section")
    selected = expert_ids[:, :, None] == jnp.arange(experts, dtype=jnp.int32)[None, None, :]
    chosen = jnp.sum(jnp.where(selected, logits[:, None, :], 0.0), axis=2)
    gates = jax.nn.sigmoid(chosen - chosen[:, ::-1])
    flat_ids = expert_ids.reshape(-1)
    onehot = (flat_ids[:, None] == jnp.arange(experts, dtype=jnp.int32)[None, :]).astype(jnp.int32)
    rank_in = jnp.sum((jnp.cumsum(onehot, axis=0) - onehot) * onehot, axis=1)
    targets = flat_ids * capacity + rank_in
    outgoing = (
        jnp.zeros((total_rows, columns), jnp.bfloat16)
        .at[targets]
        .set(jnp.repeat(activations, 2, axis=0))
    )
    outgoing = jnp.repeat(outgoing.reshape(experts, capacity, columns), quarters, axis=0)
    received = lax.all_to_all(outgoing, "expert", split_axis=0, concat_axis=0, tiled=True)
    senders = received.shape[0]
    items = received.shape[1]
    rows = received.reshape(senders * items, columns)
    pre_part = lax.dot_general(
        rows, w_up, (((1,), (1,)), ((), ())), preferred_element_type=jnp.float32
    )
    whole = lax.psum(pre_part.astype(jnp.bfloat16), "section").astype(jnp.float32)
    hidden = jax.nn.silu(whole).astype(jnp.bfloat16)
    result = jnp.dot(hidden, w_down, preferred_element_type=jnp.float32)
    result = result.astype(jnp.bfloat16).reshape(senders, items, columns)
    returned = lax.all_to_all(result, "expert", split_axis=0, concat_axis=0, tiled=True)
    returned = (
        returned.reshape(experts, quarters, capacity, columns)
        .transpose(1, 0, 2, 3)
        .reshape(quarters, total_rows, columns)
    )
    picked = jnp.sum(returned[:, targets].astype(jnp.float32), axis=0)
    picked = picked.reshape(tok_rows, 2, columns)
    mixed = activations.astype(jnp.float32) + jnp.sum(gates[:, :, None] * picked, axis=1)
    return mixed.astype(jnp.bfloat16)


def solution(mesh):
    placed = (
        P("expert", "section"),
        P(None, "section"),
        P("expert", "section"),
        P("expert", "section"),
        P("expert", None),
    )
    return jax.shard_map(
        body, mesh=mesh, in_specs=placed, out_specs=P("expert", "section"), check_vma=False
    )
```

profile of v0, /device:TPU:0, one launch (start us, length us, event | category | flops | bytes accessed | tf_op | source)
XLA Modules:
  0.0 319.1 jit_solution(5644687808206776180)
XLA Ops:
  6.5 0.0 copy-start
  6.5 0.0 all-reduce.2.cloned.1.call-start
  6.5 0.8 copy.15
  7.4 0.1 eq.45
  7.5 0.1 eq.41
  7.7 0.7 broadcast_multiply_fusion
  8.3 1.1 reduce-window.6
  9.5 0.2 slice_reduce_fusion
  9.7 0.1 copy.14
  9.9 0.1 mul.38
  10.0 1.9 broadcast_in_dim.28
  12.0 0.6 reshape.89
  12.6 0.1 fusion.13
  12.7 3.4 %scatter_custom_fusion = bf16[512,1536]{1,0:T(8,128)(2,1)S(1)} fusion(s32[512]{0:T(512)S(1)} %bitcast.23, bf16[512,1536]{1,0:T(8,128)(2,1)S(1)} %reshape.89, bf16[]{:T(256)} %constant.4.clone.1), kind=kCustom, calls=%fused_computation.14 | custom fusion | bytes 1572866 | tf_op jit(solution)/shard_map/scatter | solution.py:29
  16.2 44.1 %all_to_all.10 = bf16[8,64,1536]{2,1,0:T(8,128)(2,1)S(1)} all-to-all(bf16[8,64,1536]{2,1,0:T(8,128)(2,1)S(1)} %bitcast.20), channel_id=1, replica_groups=mesh['section'=4,'expert'=8] {'expert'}, dimensions={0} | all-to-all | bytes 3145728 | tf_op jit(solution)/shard_map/all_to_all | solution.py:32
  60.2 19.0 %convolution_convert_fusion = bf16[512,8192]{1,0:T(8,128)(2,1)} fusion(bf16[512,1536]{1,0:T(8,128)(2,1)S(1)} %bitcast.22, bf16[8192,1536]{1,0:T(8,128)(2,1)} %param.7), kind=kOutput, calls=%fused_computation.8 | convolution fusion | flops 12889096192 | bytes 35127296 | tf_op jit(solution)/shard_map/dot_general | solution.py:36
  79.2 0.0 all-reduce.2.cloned.1.call-update
  79.2 152.1 %all-reduce.2.cloned.1.call-done = bf16[512,8192]{1,0:T(8,128)(2,1)} async-done(((bf16[512,8192]{1,0:T(8,128)(2,1)}), bf16[512,8192]{1,0:T(8,128)(2,1)}) %all-reduce.2.cloned.1.call-update) | async-done | bytes 8388624 | tf_op jit(solution)/shard_map/psum | solution.py:39
  231.3 25.9 %fusion.7 = bf16[512,1536]{1,0:T(8,128)(2,1)} fusion(bf16[8192,1536]{1,0:T(8,128)(2,1)} %param.8, bf16[512,8192]{1,0:T(8,128)(2,1)} %all-reduce.2.cloned.1.call-done), kind=kOutput, calls=%fused_computation.12 | convolution fusion | flops 12910854144 | bytes 35127296 | tf_op jit(solution)/shard_map/dot_general | solution.py:41
  257.1 0.0 copy-start.1
  257.2 0.0 copy-start.3
  257.2 5.6 %all-to-all-start.1 = ((bf16[8,64,1536]{2,1,0:T(8,128)(2,1)}), bf16[8,64,1536]{2,1,0:T(8,128)(2,1)S(1)}, u32[]{:S(2)}, u32[]{:S(2)}) async-start(bf16[8,64,1536]{2,1,0:T(8,128)(2,1)} %bitcast.21), calls=%async_computation.1 | async-start | bytes 3145728 | tf_op jit(solution)/shard_map/all_to_all | solution.py:43
  262.8 0.0 copy-done
  262.8 0.0 copy-done.1
  262.8 0.3 fusion.16
  263.1 6.3 %psum.14 = f32[256,8]{0,1:T(8,128)S(1)} all-reduce(f32[256,8]{0,1:T(8,128)S(1)} %fusion.16), channel_id=1, replica_groups=mesh['section'=4,'expert'=8] {'section'}, use_global_device_ids=true, to_apply=%region_0.0 | all-reduce | flops 2048 | bytes 16384 | tf_op jit(solution)/shard_map/psum | solution.py:18
  269.4 0.0 copy-done.3
  269.4 0.1 rev.3
  269.5 0.1 copy.13
  269.7 30.0 %all-to-all-done.1 = bf16[8,64,1536]{2,1,0:T(8,128)(2,1)S(1)} async-done(((bf16[8,64,1536]{2,1,0:T(8,128)(2,1)}), bf16[8,64,1536]{2,1,0:T(8,128)(2,1)S(1)}, u32[]{:S(2)}, u32[]{:S(2)}) %all-to-all-start.1) | async-done | bytes 1572896 | tf_op jit(solution)/shard_map/all_to_all | solution.py:43
  299.7 2.9 gather_fusion
  302.6 3.5 %reshape.74 = f32[256,2,1536]{2,1,0:T(2,128)S(1)} reshape(bf16[512,1536]{1,0:T(8,128)(2,1)} %gather_fusion) | data formatting | bytes 4718592 | tf_op jit(solution)/shard_map/convert_element_type | solution.py:49
  306.1 0.0 copy-start.2
  306.1 5.0 %multiply_reduce_fusion = f32[256,1536]{1,0:T(8,128)S(1)} fusion(f32[256,2,1536]{2,1,0:T(2,128)S(1)} %reshape.74, f32[256,2]{1,0:T(8,128)S(1)} %copy.13), kind=kLoop, calls=%fused_computation.11 | loop fusion | flops 1179648 | bytes 4720640 | tf_op jit(solution)/shard_map/reduce_sum | solution.py:51
  311.1 0.0 copy-done.2
  311.1 1.1 add_convert_fusion
  (7 shorter events, 0.1 us)
Async XLA Ops:
  6.5 256.3 %copy-start = (bf16[8,1536]{1,0:T(8,128)(2,1)S(1)}, bf16[8,1536]{1,0:T(8,128)(2,1)}, u32[]{:S(2)}) copy-start(bf16[8,1536]{1,0:T(8,128)(2,1)} %param.6) | copy-start | bytes 73732
  6.5 224.7 %all-reduce.2.cloned.1.call-start = ((), (), s32[]{:S(2)}) async-start(), calls=%async_computation.2 | async-start | bytes 16777216 | tf_op jit(solution)/shard_map/psum | solution.py:39
  257.1 5.7 %copy-start.1 = (bf16[256,1536]{1,0:T(8,128)(2,1)S(1)}, bf16[256,1536]{1,0:T(8,128)(2,1)}, u32[]{:S(2)}) copy-start(bf16[256,1536]{1,0:T(8,128)(2,1)} %param.5) | copy-start | bytes 2359300
  257.2 12.2 %copy-start.3 = (s32[256,2]{0,1:T(2,128)S(1)}, s32[256,2]{0,1:T(2,128)}, u32[]{:S(2)}) copy-start(s32[256,2]{0,1:T(2,128)} %param.9) | copy-start | bytes 6148
  257.2 42.5 %all-to-all-start.1 = ((bf16[8,64,1536]{2,1,0:T(8,128)(2,1)}), bf16[8,64,1536]{2,1,0:T(8,128)(2,1)S(1)}, u32[]{:S(2)}, u32[]{:S(2)}) async-start(bf16[8,64,1536]{2,1,0:T(8,128)(2,1)} %bitcast.21), calls=%async_computation.1 | async-start | bytes 3145728 | tf_op jit(solution)/shard_map/all_to_all | solution.py:43
  306.1 5.0 %copy-start.2 = (bf16[256,1536]{1,0:T(8,128)(2,1)S(1)}, bf16[256,1536]{1,0:T(8,128)(2,1)}, u32[]{:S(2)}) copy-start(bf16[256,1536]{1,0:T(8,128)(2,1)} %param.5) | copy-start | bytes 2359300
Sparse Core Ops, SparseCore 0:
  79.3 151.8 all-reduce.1
where the time goes:
time: 319 us
  waiting for transfers between devices  182 us (57%)
  blocking collectives  50.3 us (16%)
  matrix products  45.1 us (14%)
  local copies, waits for them, and re-layouts  14.3 us (4%)
  between operations  13.5 us (4%)
  other arithmetic  8.06 us (3%)
  starting transfers between devices  5.65 us (2%)
    psum x1, waiting for transfers between devices, body(): lax.psum(pre_part.astype(jnp.bfloat16), 'section').astype(jnp.float32)  152 us
    all_to_all x1, blocking collectives, body(): lax.all_to_all(outgoing, 'expert', split_axis=0, concat_axis=0, tiled=True)  44.1 us
    all_to_all x1, waiting for transfers between devices, body(): lax.all_to_all(result, 'expert', split_axis=0, concat_axis=0, tiled=True)  30 us
    dot_general x1, matrix products, body(): result = jnp.dot(hidden, w_down, preferred_element_type=jnp.float32)  25.9 us
    dot_general x1, matrix products, body(): lax.dot_general(rows, w_up, (((1,), (1,)), ((), ())), preferred_element_t...  19 us
  transfers between devices with their start and end apart: 2, of which 2 were waited for; matrix products, arithmetic and copies ran while one was open for 0% of the time, Pallas kernels for 0%

commit v1 on v0

v1 whole, which is shorter than its diff:
```python
import functools

import jax
import jax.numpy as jnp
from jax import lax
from jax.experimental import pallas as pl
from jax.experimental.pallas import tpu as pltpu
from jax.sharding import PartitionSpec as P

BF = jnp.bfloat16
F32 = jnp.float32
VM = pl.BlockSpec(memory_space=pltpu.VMEM)
ANY = pl.BlockSpec(memory_space=pl.ANY)
HBM = pl.BlockSpec(memory_space=pltpu.HBM)
LONG = pl.CostEstimate(flops=10**12, bytes_accessed=1, transcendentals=0)
COST = pl.CostEstimate(flops=1, bytes_accessed=1, transcendentals=0)
SM = pl.BlockSpec(memory_space=pltpu.SMEM)
TILE = 512
SLOTS = 4
NP = 4
LIMIT = 40


def kernel_call(kernel, **options):
    return pl.pallas_call(kernel, **{"cost_estimate": COST, **options})


def sds(shape, dtype=BF):
    return jax.ShapeDtypeStruct(shape, dtype)


def params(mib):
    return pltpu.CompilerParams(vmem_limit_bytes=mib << 20)


def plain(activations, router_weight, w_up, w_down, expert_ids):
    group = lax.axis_size("expert")
    experts = router_weight.shape[0]
    quarters = group // experts
    tok_rows, columns = activations.shape
    capacity = tok_rows // 4
    total_rows = experts * capacity
    logits = lax.psum(
        lax.dot_general(
            activations, router_weight, (((1,), (1,)), ((), ())), preferred_element_type=F32
        ),
        "section",
    )
    selected = expert_ids[:, :, None] == jnp.arange(experts, dtype=jnp.int32)[None, None, :]
    chosen = jnp.sum(jnp.where(selected, logits[:, None, :], 0.0), axis=2)
    gates = jax.nn.sigmoid(chosen - chosen[:, ::-1])
    flat_ids = expert_ids.reshape(-1)
    onehot = flat_ids[:, None] == jnp.arange(experts, dtype=jnp.int32)[None, :]
    places = jnp.arange(flat_ids.shape[0])
    before = (places[None, :] < places[:, None]).astype(BF)
    counts = jnp.dot(before, onehot.astype(BF), preferred_element_type=F32)
    rank_in = jnp.sum(jnp.where(onehot, counts, 0.0), axis=1).astype(jnp.int32)
    targets = flat_ids * capacity + rank_in
    outgoing = (
        jnp.zeros((total_rows, columns), BF).at[targets].set(jnp.repeat(activations, 2, axis=0))
    )
    outgoing = jnp.repeat(outgoing.reshape(experts, capacity, columns), quarters, axis=0)
    received = lax.all_to_all(outgoing, "expert", split_axis=0, concat_axis=0, tiled=True)
    senders, items = received.shape[:2]
    rows = received.reshape(senders * items, columns)
    pre_part = lax.dot_general(rows, w_up, (((1,), (1,)), ((), ())), preferred_element_type=F32)
    whole = lax.psum(pre_part.astype(BF), "section").astype(F32)
    hidden = jax.nn.silu(whole).astype(BF)
    result = jnp.dot(hidden, w_down, preferred_element_type=F32)
    result = result.astype(BF).reshape(senders, items, columns)
    returned = lax.all_to_all(result, "expert", split_axis=0, concat_axis=0, tiled=True)
    returned = (
        returned.reshape(experts, quarters, capacity, columns)
        .transpose(1, 0, 2, 3)
        .reshape(quarters, total_rows, columns)
    )
    onehot = (targets[:, None] == jnp.arange(total_rows)[None, :]).astype(BF)
    picked = jnp.einsum("ts,qsd->td", onehot, returned, preferred_element_type=F32)
    picked = picked.reshape(tok_rows, 2, columns)
    mixed = activations.astype(F32) + jnp.sum(gates[:, :, None] * picked, axis=1)
    return mixed.astype(BF)


PARTS = 8


def cut_copies(first, core, half, w_ref, o_ref, hold, sem):
    step = o_ref.shape[0] // PARTS
    start = pl.multiple_of((1 - core) * half + first, step)
    ins = [
        pltpu.make_async_copy(w_ref.at[pl.ds(start + i * step, step), :], hold.at[i], sem.at[i])
        for i in range(PARTS)
    ]
    outs = [
        pltpu.make_async_copy(hold.at[i], o_ref.at[pl.ds(i * step, step), :], sem.at[PARTS + i])
        for i in range(PARTS)
    ]
    return ins, outs


def pack_kernel(cap, peers, me_ref, a_ref, t_ref, *outs):
    low = me_ref[0]
    per = len(peers) // len(outs)
    for i, j in enumerate(peers):
        at = i % per * cap
        outs[i // per][at : at + cap, :] = a_ref[low ^ j]


def cut_kernel(first, half, me_ref, w_ref, t_ref, o_ref, hold, sem):
    ins, outs = cut_copies(first, me_ref[0], half, w_ref, o_ref, hold, sem)
    for c in ins:
        c.start()
    for i, o in zip(ins, outs):
        i.wait()
        o.start()
    for o in outs:
        o.wait()


def cut_scratch(rows, columns):
    return [
        pltpu.VMEM((PARTS, rows // PARTS, columns), BF),
        pltpu.SemaphoreType.DMA((2 * PARTS,)),
    ]


def route_kernel(cap, me_ref, ids_ref, act_ref, router_ref, *outs):
    slot_ref, logit_ref, near_ref, all_ref = outs
    experts = router_ref.shape[0]
    tokens = act_ref.shape[0]
    low = me_ref[0] & 3
    ids = ids_ref[...] ^ me_ref[0]
    id0, id1 = ids[0:1, :], ids[1:2, :]
    line = lax.broadcasted_iota(jnp.int32, (experts, tokens), 0)
    is0, is1 = line == id0, line == id1
    member = (is0 | is1).astype(F32).astype(BF)
    r = lax.broadcasted_iota(jnp.int32, (tokens, tokens), 0)
    c = lax.broadcasted_iota(jnp.int32, (tokens, tokens), 1)
    rank = jnp.dot(member, (r < c).astype(F32).astype(BF), preferred_element_type=F32)
    first = line.astype(F32) * cap + rank
    slot0 = jnp.sum(jnp.where(is0, first, 0.0), axis=0, keepdims=True)
    slot1 = jnp.sum(jnp.where(is1, first, 0.0), axis=0, keepdims=True)
    slot_ref[...] = jnp.concatenate([slot0, slot1] + [jnp.zeros_like(slot0)] * 6, axis=0)
    act = act_ref[...]
    i0, i1 = slot0.astype(jnp.int32), slot1.astype(jnp.int32)
    s = lax.broadcasted_iota(jnp.int32, (experts * cap, tokens), 0)
    pick = ((s == i0) | (s == i1)).astype(F32).astype(BF)
    for j in range(experts):
        rows = jnp.dot(pick[j * cap : (j + 1) * cap], act, preferred_element_type=F32).astype(BF)
        if j < 4:
            near_ref[low ^ j] = rows
        all_ref[me_ref[0] ^ j] = rows
    logit_ref[...] = lax.dot_general(
        router_ref[...], act, (((1,), (1,)), ((), ())), preferred_element_type=F32
    )


def silu_kernel(a_ref, b_ref, t_ref, o_ref):
    v = a_ref[...].astype(F32) + b_ref[...].astype(F32)
    o_ref[...] = (v / (1.0 + jnp.exp(-v))).astype(BF)


def stream(sources, count, use):
    slots = min(SLOTS, count)

    def copies(g):
        for locate, buf, sem in sources:
            ref, row = locate(g)
            yield pltpu.make_async_copy(
                ref.at[pl.ds(pl.multiple_of(row, TILE), TILE), :],
                buf.at[g % slots],
                sem.at[g % slots],
            )

    for g in range(slots):
        for c in copies(g):
            c.start()
    for g in range(count):
        for c in copies(g):
            c.wait()
        use(g, *[buf.at[g % slots] for _, buf, _ in sources])
        if g + slots < count:
            for c in copies(g + slots):
                c.start()


def up_kernel(half, span, pieces, n_x, corners, me_ref, *refs):
    mine_refs, their_refs = refs[:n_x], refs[n_x : 2 * n_x]
    w_ref, *got_refs = refs[2 * n_x : 2 * n_x + 3]
    n_p = len(pieces)
    x, y, buf_a, sem_a, buf_b, sem_b = refs[-6:]
    core = me_ref[0]
    out_refs = refs[-6 - len(corners) : -6]
    rows = mine_refs[0].shape[0]
    for i in range(n_x):
        x[i * rows : (i + 1) * rows, :] = mine_refs[i][...]
        y[i * rows : (i + 1) * rows, :] = their_refs[i][1 - core]
    each = span // TILE

    def locate_a(g):
        return w_ref, core * half + pieces[g // each] * span + (g % each) * TILE

    def locate_b(g):
        row = pieces[g // each] * span + (g % each) * TILE
        return got_refs[row // (half // 2)], row % (half // 2)

    dims = (((1,), (1,)), ((), ()))

    def use(g, a, b):
        v = (
            lax.dot_general(x[...], a[...], dims, preferred_element_type=F32)
            + lax.dot_general(y[...], b[...], dims, preferred_element_type=F32)
        ).astype(BF)
        for o, (row, col) in zip(out_refs, corners):
            at = g * TILE - col
            if 0 <= at < o.shape[1]:
                o[:, at : at + TILE] = v[row : row + o.shape[0], :]

    stream([(locate_a, buf_a, sem_a), (locate_b, buf_b, sem_b)], each * n_p, use)


def down_kernel(half, plan, ready, has_acc, me_ref, *refs):
    n_in = plan[-1][1] + 1
    wide = 1 if ready else 2
    s_refs = refs[: wide * n_in]
    w_ref, got_ref = refs[wide * n_in : wide * n_in + 2]
    k = wide * n_in + 2
    acc_refs = refs[k : k + 2] if has_acc else None
    k += 1 + (2 if has_acc else 0)
    own_ref, *oth_refs = refs[k:-7]
    h, own, oth, buf_a, sem_a, buf_b, sem_b = refs[-7:]
    core = me_ref[0]

    def locate_a(g):
        return w_ref, core * half + plan[g][0]

    def locate_b(g):
        return got_ref, plan[g][0]

    def use(g, a, b):
        _, i, c = plan[g]
        cols = slice(c, c + TILE)
        if ready:
            h[...] = s_refs[i][:, cols]
        else:
            v = s_refs[2 * i][:, cols].astype(F32) + s_refs[2 * i + 1][:, cols].astype(F32)
            h[...] = (v / (1.0 + jnp.exp(-v))).astype(BF)
        for i, (total, w) in enumerate(((own, a), (oth, b))):
            part = jnp.dot(h[...], w[...], preferred_element_type=F32)
            if g == 0:
                total[...] = part + acc_refs[i][...] if has_acc else part
            else:
                total[...] += part

    stream([(locate_a, buf_a, sem_a), (locate_b, buf_b, sem_b)], len(plan), use)
    own_ref[...] = own[...]
    each = own.shape[0] // len(oth_refs)
    for i, r in enumerate(oth_refs):
        r[...] = oth[i * each : (i + 1) * each, :].astype(r.dtype)


def finish_kernel(cap, near, parts, me_ref, own_ref, *refs):
    got_refs, outs = refs[:parts], refs[parts + 1 :]
    core, low = me_ref[0], me_ref[1]
    got = jnp.concatenate([r[1 - core] for r in got_refs], axis=0)
    for i in range(own_ref.shape[0] // cap):
        rows = slice(i * cap, (i + 1) * cap)
        v = (own_ref[rows, :] + got[rows, :].astype(F32)).astype(BF)
        if near:
            outs[0][low ^ i] = v
        else:
            outs[i][...] = v


def combine_kernel(cap, peers, me_ref, ids_ref, slot_ref, logit_ref, acc_ref, *refs):
    n = 1 if peers is None else len(peers)
    r_refs = refs[:n]
    out_ref = refs[n + 1]
    experts, tokens = logit_ref.shape
    line = lax.broadcasted_iota(jnp.int32, (experts, tokens), 0)
    ids = ids_ref[...]
    logits = logit_ref[...]
    c0 = jnp.sum(jnp.where(line == ids[0:1, :], logits, 0.0), axis=0, keepdims=True)
    c1 = jnp.sum(jnp.where(line == ids[1:2, :], logits, 0.0), axis=0, keepdims=True)
    g0, g1 = jax.nn.sigmoid(c0 - c1), jax.nn.sigmoid(c1 - c0)
    flat = jnp.concatenate([g0, g1, slot_ref[0:2, :]] + [jnp.zeros_like(g0)] * 4, axis=0)
    tall = jnp.transpose(flat)
    g0, g1 = tall[:, 0:1], tall[:, 1:2]
    s0, s1 = tall[:, 2:3].astype(jnp.int32), tall[:, 3:4].astype(jnp.int32)
    if peers is None:
        blocks = [(j, r_refs[0][me_ref[1] ^ j]) for j in range(4)]
    else:
        blocks = [(j, r[...]) for j, r in zip(peers, r_refs)]
    width = cap * len(blocks)
    place = lax.broadcasted_iota(jnp.int32, (tokens, width), 1)
    shift = jnp.zeros((tokens, width), jnp.int32)
    for i, (j, _) in enumerate(blocks):
        inside = (place >= i * cap) & (place < (i + 1) * cap)
        shift = jnp.where(inside, (j - i) * cap, shift)
    place = place + shift
    q0 = (place == s0).astype(F32).astype(BF)
    q1 = (place == s1).astype(F32).astype(BF)
    rows = jnp.concatenate([b for _, b in blocks], axis=0)
    total = (
        acc_ref[...].astype(F32)
        + g0 * jnp.dot(q0, rows, preferred_element_type=F32)
        + g1 * jnp.dot(q1, rows, preferred_element_type=F32)
    )
    out_ref[...] = total.astype(out_ref.dtype)


CHUNKS = ((), (0, 1, 2, 3), (4, 5), (6, 7))
ORDER = (
    ("W", 0),
    ("W", 1),
    ("X", (1,)),
    ("U", (1,), (0, 1), ((1, (0, 1)),)),
    ("W", None),
    ("U", (1,), (2, 3), ((1, (2, 3)),)),
    ("X", (2, 3)),
    ("U", (2, 3), (0, 1, 2, 3), ((3, (0, 1, 2, 3)), (2, (0, 1, 2, 3)))),
    ("H", 1, (0, 1)),
    ("H", 1, (2, 3)),
    ("D", 1, (0, 1, 2, 3)),
    ("F", 1),
    ("D", 2, (0, 1, 2, 3)),
    ("F", 2),
    ("D", 3, (0, 1, 2, 3)),
    ("F", 3),
    ("C", 1),
    ("C", 2),
    ("C", 3),
)


def pipelined(activations, router_weight, w_up, w_down, expert_ids):
    experts = router_weight.shape[0]
    tokens, columns = activations.shape
    cap = tokens // 4
    half = w_up.shape[0] // 2
    span = half // NP
    section = lax.axis_index("section").astype(jnp.int32)
    place = lax.axis_index("expert").astype(jnp.int32)
    me = jnp.stack([section % 2, place & 3])
    swap_core = [(i, i ^ 1) for i in range(4)]
    swap_y = [(i, i ^ 2) for i in range(4)]
    groups = [[0, 1, 2, 3], [4, 5, 6, 7]]

    def peer(j):
        return [(i, i ^ j) for i in range(experts)]

    def core_swap(v):
        return lax.ppermute(v, "section", swap_core)

    def core_pair(v):
        return lax.all_gather(v, "section", axis_index_groups=[[0, 1], [2, 3]])

    def near_swap(v):
        return lax.all_to_all(
            v, "expert", split_axis=0, concat_axis=0, axis_index_groups=groups, tiled=True
        )

    ids = expert_ids.T
    slots, logits, near_rows, all_rows = kernel_call(
        functools.partial(route_kernel, cap),
        out_shape=[sds((8, tokens), F32), sds((experts, tokens), F32)]
        + [sds((4, cap, columns)), sds((experts, cap, columns))],
        in_specs=[SM, VM, VM, VM],
        out_specs=[VM] * 4,
        compiler_params=params(LIMIT),
        name="route",
    )(place.reshape(1), ids, activations, router_weight)
    near = near_swap(near_rows)
    far = lax.all_to_all(all_rows, "expert", split_axis=0, concat_axis=0, tiled=True)
    mine_x, their_x = {}, {}
    tok = slots
    logits = logits + core_swap(logits)
    logits = logits + lax.ppermute(logits, "section", swap_y)
    w_up2, w_down2 = {}, None

    def cut(i):
        nonlocal tok, w_down2
        rows = half if i is None else half // 2
        tok = kernel_call(
            functools.partial(cut_kernel, i * rows if i else 0, half),
            out_shape=sds((rows, columns)),
            in_specs=[SM, HBM, ANY],
            out_specs=HBM,
            scratch_shapes=cut_scratch(rows, columns),
            compiler_params=params(LIMIT),
            name=f"cut{i}",
        )(me, w_down if i is None else w_up, tok)
        if i is None:
            w_down2 = core_swap(tok)
        else:
            w_up2[i] = core_swap(tok)

    sums, back, partial = {}, {}, {}

    def pack(chunks):
        nonlocal tok
        peers = [j for c in chunks for j in CHUNKS[c]]
        res = kernel_call(
            functools.partial(pack_kernel, cap, peers),
            out_shape=[sds((2 * cap, columns))] * 2,
            in_specs=[SM, VM, ANY],
            out_specs=[VM] * 2,
            compiler_params=params(LIMIT),
            cost_estimate=LONG if chunks == (1,) else COST,
            name=f"pack{chunks[0]}",
        )(
            (place & 3 if chunks == (1,) else place).reshape(1),
            near if chunks == (1,) else far,
            tok,
        )
        tok = res[0]
        mine_x[chunks], their_x[chunks] = res, [core_pair(r) for r in res]

    def absorb(c, pieces):
        nonlocal tok
        pair = sums[c, pieces[0]][0]
        tok = kernel_call(
            silu_kernel,
            out_shape=sds(pair[0].shape),
            in_specs=[VM, VM, ANY],
            out_specs=VM,
            compiler_params=params(LIMIT),
            cost_estimate=LONG,
            name=f"silu{c}",
        )(*pair, tok)
        for p in pieces:
            sums[c, p] = (tok, sums[c, p][1])

    def slots_of(n):
        return [
            pltpu.VMEM((min(SLOTS, n), TILE, columns), BF),
            pltpu.SemaphoreType.DMA((min(SLOTS, n),)),
        ] * 2

    def up(chunks, pieces, places):
        nonlocal tok
        n = cap * sum(len(CHUNKS[c]) for c in chunks)
        mine, theirs = mine_x[chunks], their_x[chunks]
        got = (w_up2[0], w_up2[pieces[-1] * 2 // NP])
        rows = {c: cap * sum(len(CHUNKS[d]) for d in chunks if d < c) for c in chunks}
        corners = [(rows[c], (ps[0] - pieces[0]) * span) for c, ps in places]
        outs = kernel_call(
            functools.partial(up_kernel, half, span, pieces, len(mine), corners),
            out_shape=[sds((cap * len(CHUNKS[c]), span * len(ps))) for c, ps in places],
            in_specs=[SM] + [VM] * (len(mine) + len(theirs)) + [HBM, ANY, ANY, ANY, ANY],
            out_specs=[VM] * len(places),
            scratch_shapes=[pltpu.VMEM((n, columns), BF)] * 2
            + slots_of(span * len(pieces) // TILE),
            compiler_params=params(LIMIT),
            name="up" + "".join(map(str, chunks)) + f"_{pieces[0]}",
        )(me, *mine, *theirs, w_up, *got, tok, logits)
        tok = outs[0]
        for (c, ps), out in zip(places, outs):
            pair = (out, lax.ppermute(out, "section", swap_y))
            for i, p in enumerate(ps):
                sums[c, p] = (pair, i * span)

    def down(c, pieces, final):
        nonlocal tok
        held = [p for p in pieces if not isinstance(sums[c, p][0], tuple)]
        if held and len(held) < len(pieces):
            down(c, held, False)
            pieces = [p for p in pieces if p not in held]
        ready = not isinstance(sums[c, pieces[0]][0], tuple)
        arrays, plan = [], []
        for p in pieces:
            pair, at = sums[c, p]
            if not arrays or arrays[-1] is not pair:
                arrays.append(pair)
            plan += [(p * span + t, len(arrays) - 1, at + t) for t in range(0, span, TILE)]
        flat = arrays if ready else [v for pair in arrays for v in pair]
        n = cap * len(CHUNKS[c])
        acc = partial.get(c, ())
        parts = 2 if final and c == 1 else 1
        res = kernel_call(
            functools.partial(down_kernel, half, plan, ready, len(acc) > 0),
            out_shape=[sds((n, columns), F32)] + [sds((n // parts, columns), BF if final else F32)] * parts,
            in_specs=[SM] + [VM] * len(flat) + [HBM, ANY] + [VM] * len(acc) + [ANY],
            out_specs=[VM] * (1 + parts),
            scratch_shapes=[
                pltpu.VMEM((n, TILE), BF),
                pltpu.VMEM((n, columns), F32),
                pltpu.VMEM((n, columns), F32),
            ]
            + slots_of(len(plan)),
            compiler_params=params(LIMIT),
            name=f"down{c}_{pieces[0]}",
        )(me, *flat, w_down, w_down2, *acc, tok)
        tok = res[0]
        partial[c] = (res[0], *[core_pair(r) for r in res[1:]]) if final else tuple(res)

    def finish(c):
        nonlocal tok
        own, *others = partial[c]
        peers = CHUNKS[c]
        near = c == 1
        res = kernel_call(
            functools.partial(finish_kernel, cap, near, len(others)),
            out_shape=[sds((4, cap, columns))] if near else [sds((cap, columns))] * len(peers),
            in_specs=[SM] + [VM] * (1 + len(others)) + [ANY],
            out_specs=[VM] * (1 if near else len(peers)),
            compiler_params=params(LIMIT),
            name=f"finish{c}",
        )(me, own, *others, tok)
        tok = res[0]
        if near:
            back[1] = [near_swap(res[0])]
        else:
            back[c] = [r if j == 0 else lax.ppermute(r, "expert", peer(j)) for j, r in zip(peers, res)]

    total = activations

    def combine(c, final):
        nonlocal tok, total
        total = tok = kernel_call(
            functools.partial(combine_kernel, cap, None if c == 1 else CHUNKS[c]),
            out_shape=sds((tokens, columns), BF if final else F32),
            in_specs=[SM] + [VM] * (4 + len(back[c])) + [ANY],
            out_specs=VM,
            compiler_params=params(LIMIT),
            name=f"combine{c}",
        )(me, ids, slots, logits, total, *back[c], tok)

    for i, (kind, n, *rest) in enumerate(ORDER):
        if kind == "W":
            cut(n)
        elif kind == "X":
            pack(n)
        elif kind == "U":
            up(n, *rest)
        elif kind == "H":
            absorb(n, *rest)
        elif kind == "D":
            down(n, rest[0], rest[0][-1] == NP - 1)
        elif kind == "F":
            finish(n)
        else:
            combine(n, i == len(ORDER) - 1)
    return total


def body(activations, router_weight, w_up, w_down, expert_ids):
    if (
        lax.axis_size("section") == 4
        and lax.axis_size("expert") == router_weight.shape[0] == 8
        and activations.shape[0] == 256
    ):
        return pipelined(activations, router_weight, w_up, w_down, expert_ids)
    return plain(activations, router_weight, w_up, w_down, expert_ids)


def solution(mesh):
    placed = (
        P("expert", "section"),
        P(None, "section"),
        P("expert", "section"),
        P("expert", "section"),
        P("expert", None),
    )
    return jax.shard_map(
        body, mesh=mesh, in_specs=placed, out_specs=P("expert", "section"), check_vma=False
    )
```

time: 319 us -> 177 us (0.55)
  the two profiles are of different devices: /device:TPU:0 before, /device:TPU:16 now
where the time goes in v1:
time: 177 us; the launch traced here: 176 us
  Pallas kernels  94.6 us (53%)
  blocking collectives  30.1 us (17%)
  starting transfers between devices  29.1 us (16%)
  waiting for transfers between devices  19.7 us (11%)
  local copies, waits for them, and re-layouts  2.58 us (1%)
    pallas_call x3, Pallas kernels, down(): kernel_call(functools.partial(down_kernel, half, plan, ready, len(acc) >...  31.7 us
    all_gather x8, blocking collectives, core_pair(): return lax.all_gather(v, 'section', axis_index_groups=[[0, 1], [2, 3]])  30.1 us
    pallas_call x3, Pallas kernels, up(): kernel_call(functools.partial(up_kernel, half, span, pieces, len(mine), c...  25.9 us
    pallas_call x3, Pallas kernels, cut(): kernel_call(functools.partial(cut_kernel, i * rows if i else 0, half), ou...  22.1 us
    ppermute x4, waiting for transfers between devices, finish(): lax.ppermute(r, 'expert', peer(j))  14.7 us
    ppermute x4, starting transfers between devices, finish(): lax.ppermute(r, 'expert', peer(j))  8.08 us
    all_to_all x2, starting transfers between devices, near_swap(): lax.all_to_all(v, 'expert', split_axis=0, concat_axis=0, axis_index_group...  7.96 us
    all_to_all x1, starting transfers between devices, pipelined(): lax.all_to_all(all_rows, 'expert', split_axis=0, concat_axis=0, tiled=True)  6.57 us
  transfers between devices with their start and end apart: 16, of which 5 were waited for; matrix products, arithmetic and copies ran while one was open for 0% of the time, Pallas kernels for 51%

profile of v1, /device:TPU:16, one launch (start us, length us, event | category | flops | bytes accessed | tf_op | source)
XLA Modules:
  0.0 176.4 jit_solution(10726790188094392339)
XLA Ops:
  0.0 1.1 copy-done
  1.1 0.7 copy-done.9
  1.8 0.7 copy-done.11
  2.6 2.7 %route.1 = (f32[8,256]{1,0:T(8,128)S(1)}, f32[8,256]{1,0:T(8,128)S(1)}, bf16[4,64,1536]{2,1,0:T(8,128)(2,1)}, bf16[8,64,1536]{2,1,0:T(8,128)(2,1)}) custom-call(s32[1]{0:T(128)} %bitcast.3.me_ref, s32[2,256]{1,0:T(2,128)S(1)} %bitcast.22, bf16[256,1536]{1,0:T(8,128)(2,1)S(1)} %copy-done, bf16[8,1536]{1,0:T(8,128)(2,1)S(1)} %copy-done.11), custom_call_target="tpu_custom_call" | custom-call | flops 1 | bytes 1 | tf_op jit(solution)/shard_map/route/pallas_call | solution.py:364
  5.3 3.8 %all-to-all-start = ((bf16[4,64,1536]{2,1,0:T(8,128)(2,1)}), bf16[4,64,1536]{2,1,0:T(8,128)(2,1)S(1)}, u32[]{:S(2)}, u32[]{:S(2)}) async-start(bf16[4,64,1536]{2,1,0:T(8,128)(2,1)} %get-tuple-element.28), calls=%async_computation | async-start | bytes 1572864 | tf_op jit(solution)/shard_map/all_to_all | solution.py:359
  9.0 0.0 collective-permute-start
  9.0 1.2 collective-permute-done
  10.2 1.5 collective-permute-start.1
  11.7 0.1 pad_add_fusion.me_ref
  11.8 6.1 %cut0.1.t_ref = bf16[2048,1536]{1,0:T(8,128)(2,1)} custom-call(s32[2]{0:T(128)S(1)} %pad_add_fusion.me_ref, bf16[8192,1536]{1,0:T(8,128)(2,1)} %refs_4_.5, f32[8,256]{1,0:T(8,128)S(1)} %get-tuple-element.26.t_ref.slot_ref), custom_call_target="tpu_custom_call" | custom-call | flops 1 | bytes 1 | tf_op jit(solution)/shard_map/cut0/pallas_call | solution.py:384
  17.9 0.1 collective-permute-start.2
  18.0 6.1 %cut1.1.t_ref = bf16[2048,1536]{1,0:T(8,128)(2,1)} custom-call(s32[2]{0:T(128)S(1)} %pad_add_fusion.me_ref, bf16[8192,1536]{1,0:T(8,128)(2,1)} %refs_4_.5, bf16[2048,1536]{1,0:T(8,128)(2,1)} %cut0.1.t_ref), custom_call_target="tpu_custom_call" | custom-call | flops 1 | bytes 1 | tf_op jit(solution)/shard_map/cut1/pallas_call | solution.py:384
  24.1 0.6 collective-permute-start.4
  24.6 0.0 collective-permute-done.1
  24.6 0.0 all-to-all-done.a_ref
  24.6 6.6 %all-to-all-start.1 = ((bf16[8,64,1536]{2,1,0:T(8,128)(2,1)}), bf16[8,64,1536]{2,1,0:T(8,128)(2,1)}, u32[]{:S(2)}, u32[]{:S(2)}) async-start(bf16[8,64,1536]{2,1,0:T(8,128)(2,1)} %get-tuple-element.31), calls=%async_computation.1 | async-start | bytes 3145728 | tf_op jit(solution)/shard_map/all_to_all | solution.py:374
  31.2 0.1 pack1.1
  31.3 6.4 %all-gather = bf16[256,1536]{1,0:T(8,128)(2,1)S(1)} all-gather(bf16[128,1536]{1,0:T(8,128)(2,1)S(1)} %get-tuple-element.29.refs_0_.refs_7_), channel_id=2, replica_groups={{0,8},{16,24},{1,9},{17,25},{2,10},{18,26},{3,11},{19,27},{4,12},{20,28..., dimensions={0}, use_global_device_ids=true | all-gather | bytes 1179648 | tf_op jit(solution)/shard_map/all_gather | solution.py:356
  37.7 2.4 %all-gather.1 = bf16[256,1536]{1,0:T(8,128)(2,1)S(1)} all-gather(bf16[128,1536]{1,0:T(8,128)(2,1)S(1)} %get-tuple-element.30.refs_1_), channel_id=3, replica_groups={{0,8},{16,24},{1,9},{17,25},{2,10},{18,26},{3,11},{19,27},{4,12},{20,28..., dimensions={0}, use_global_device_ids=true | all-gather | bytes 1179648 | tf_op jit(solution)/shard_map/all_gather | solution.py:356
  40.0 0.0 collective-permute-done.2.refs_5_.refs_6_
  40.0 6.5 %up1_0.1.t_ref.a_ref = bf16[256,2048]{1,0:T(8,128)(2,1)S(1)} custom-call(s32[2]{0:T(128)S(1)} %copy-done.7, bf16[128,1536]{1,0:T(8,128)(2,1)S(1)} %get-tuple-element.29.refs_0_.refs_7_, bf16[128,1536]{1,0:T(8,128)(2,1)S(1)} %get-tuple-element.30.refs_1_, bf16[2,128,1536]{2,1,0:T(8,128)(2,1)S(1)} %bitcast.12, bf16[2,128,1536]{2,1,0:T(8,128)(2,1)S(1)} %bitcast.14, ...), custom_call_target="tpu_custom_call" | custom-call | flops 1 | bytes 1 | tf_op jit(solution)/shard_map/up1_0/pallas_call | solution.py:447
  46.6 0.6 collective-permute-start.3
  47.2 10.0 %cutNone.1.refs_7_ = bf16[4096,1536]{1,0:T(8,128)(2,1)} custom-call(s32[2]{0:T(128)S(1)} %copy-done.7, bf16[8192,1536]{1,0:T(8,128)(2,1)} %refs_2_.5, bf16[256,2048]{1,0:T(8,128)(2,1)S(1)} %up1_0.1.t_ref.a_ref), custom_call_target="tpu_custom_call" | custom-call | flops 1 | bytes 1 | tf_op jit(solution)/shard_map/cutNone/pallas_call | solution.py:384
  57.1 0.1 collective-permute-start.6
  57.2 0.0 collective-permute-done.4.refs_6_
  57.2 7.5 %up1_2.1.t_ref.a_ref = bf16[256,2048]{1,0:T(8,128)(2,1)} custom-call(s32[2]{0:T(128)S(1)} %copy-done.7, bf16[128,1536]{1,0:T(8,128)(2,1)S(1)} %get-tuple-element.29.refs_0_.refs_7_, bf16[128,1536]{1,0:T(8,128)(2,1)S(1)} %get-tuple-element.30.refs_1_, bf16[2,128,1536]{2,1,0:T(8,128)(2,1)S(1)} %bitcast.13, bf16[2,128,1536]{2,1,0:T(8,128)(2,1)S(1)} %bitcast.15, ...), custom_call_target="tpu_custom_call" | custom-call | flops 1 | bytes 1 | tf_op jit(solution)/shard_map/up1_2/pallas_call | solution.py:447
  64.8 1.6 collective-permute-start.5
  66.4 0.0 all-to-all-done.1.a_ref
  66.4 1.5 pack2.1
  67.8 9.1 %all-gather.2 = bf16[256,1536]{1,0:T(8,128)(2,1)S(1)} all-gather(bf16[128,1536]{1,0:T(8,128)(2,1)S(1)} %get-tuple-element.32.refs_0_.refs_7_), channel_id=4, replica_groups={{0,8},{16,24},{1,9},{17,25},{2,10},{18,26},{3,11},{19,27},{4,12},{20,28..., dimensions={0}, use_global_device_ids=true | all-gather | bytes 1179648 | tf_op jit(solution)/shard_map/all_gather | solution.py:356
  76.9 2.5 %all-gather.3 = bf16[256,1536]{1,0:T(8,128)(2,1)S(1)} all-gather(bf16[128,1536]{1,0:T(8,128)(2,1)S(1)} %get-tuple-element.33.refs_1_), channel_id=5, replica_groups={{0,8},{16,24},{1,9},{17,25},{2,10},{18,26},{3,11},{19,27},{4,12},{20,28..., dimensions={0}, use_global_device_ids=true | all-gather | bytes 1179648 | tf_op jit(solution)/shard_map/all_gather | solution.py:356
  79.5 11.9 %up23_0.1 = (bf16[128,4096]{1,0:T(8,128)(2,1)}, bf16[128,4096]{1,0:T(8,128)(2,1)}) custom-call(s32[2]{0:T(128)S(1)} %copy-done.7, bf16[128,1536]{1,0:T(8,128)(2,1)S(1)} %get-tuple-element.32.refs_0_.refs_7_, bf16[128,1536]{1,0:T(8,128)(2,1)S(1)} %get-tuple-element.33.refs_1_, bf16[2,128,1536]{2,1,0:T(8,128)(2,1)S(1)} %bitcast.20, ...), custom_call_target="tpu_custom_call" | custom-call | flops 1 | bytes 1 | tf_op jit(solution)/shard_map/up23_0/pallas_call | solution.py:447
  91.3 1.6 collective-permute-start.8
  92.9 0.5 collective-permute-start.7
  93.4 0.0 collective-permute-done.3.b_ref
  93.4 0.7 silu1.2.t_ref.refs_0_
  94.1 0.3 collective-permute-done.5.b_ref
  94.4 2.2 %silu1.3.refs_1_.refs_4_ = bf16[256,2048]{1,0:T(8,128)(2,1)S(1)} custom-call(bf16[256,2048]{1,0:T(8,128)(2,1)} %up1_2.1.t_ref.a_ref, bf16[256,2048]{1,0:T(8,128)(2,1)} %collective-permute-done.5.b_ref, bf16[256,2048]{1,0:T(8,128)(2,1)S(1)} %silu1.2.t_ref.refs_0_), custom_call_target="tpu_custom_call" | custom-call | flops 999999995904 | bytes 1 | tf_op jit(solution)/shard_map/silu1/pallas_call | solution.py:422
  96.6 0.0 collective-permute-done.6.refs_3_
  96.6 10.4 %down1_0.1 = (f32[256,1536]{1,0:T(8,128)S(1)}, bf16[128,1536]{1,0:T(8,128)(2,1)S(1)}, bf16[128,1536]{1,0:T(8,128)(2,1)S(1)}) custom-call(s32[2]{0:T(128)S(1)} %copy-done.7, bf16[256,2048]{1,0:T(8,128)(2,1)S(1)} %silu1.2.t_ref.refs_0_, bf16[256,2048]{1,0:T(8,128)(2,1)S(1)} %silu1.3.refs_1_.refs_4_, bf16[8192,1536]{1,0:T(8,128)(2,1)} %refs_2_.5, ...), custom_call_target="tpu_custom_call" | custom-call | flops 1 | bytes 1 | tf_op jit(solution)/shard_map/down1_0/pallas_call | solution.py:480
  107.1 2.4 %all-gather.4 = bf16[256,1536]{1,0:T(8,128)(2,1)S(1)} all-gather(bf16[128,1536]{1,0:T(8,128)(2,1)S(1)} %get-tuple-element.36), channel_id=6, replica_groups={{0,8},{16,24},{1,9},{17,25},{2,10},{18,26},{3,11},{19,27},{4,12},{20,28..., dimensions={0}, use_global_device_ids=true | all-gather | bytes 1179648 | tf_op jit(solution)/shard_map/all_gather | solution.py:356
  109.4 2.6 %all-gather.5 = bf16[256,1536]{1,0:T(8,128)(2,1)S(1)} all-gather(bf16[128,1536]{1,0:T(8,128)(2,1)S(1)} %get-tuple-element.37), channel_id=7, replica_groups={{0,8},{16,24},{1,9},{17,25},{2,10},{18,26},{3,11},{19,27},{4,12},{20,28..., dimensions={0}, use_global_device_ids=true | all-gather | bytes 1179648 | tf_op jit(solution)/shard_map/all_gather | solution.py:356
  112.0 1.6 finish1.1.refs_4_
  113.6 4.2 %all-to-all-start.2 = ((bf16[4,64,1536]{2,1,0:T(8,128)(2,1)}), bf16[4,64,1536]{2,1,0:T(8,128)(2,1)S(1)}, u32[]{:S(2)}, u32[]{:S(2)}) async-start(bf16[4,64,1536]{2,1,0:T(8,128)(2,1)} %finish1.1.refs_4_), calls=%async_computation.2 | async-start | bytes 1572864 | tf_op jit(solution)/shard_map/all_to_all | solution.py:359
  117.8 0.0 collective-permute-done.8.refs_1_
  117.8 10.6 %down2_0.1 = (f32[128,1536]{1,0:T(8,128)S(1)}, bf16[128,1536]{1,0:T(8,128)(2,1)S(1)}) custom-call(s32[2]{0:T(128)S(1)} %copy-done.7, bf16[128,4096]{1,0:T(8,128)(2,1)} %get-tuple-element.38.refs_0_, bf16[128,4096]{1,0:T(8,128)(2,1)} %collective-permute-done.8.refs_1_, bf16[8192,1536]{1,0:T(8,128)(2,1)} %refs_2_.5, ...), custom_call_target="tpu_custom_call" | custom-call | flops 1 | bytes 1 | tf_op jit(solution)/shard_map/down2_0/pallas_call | solution.py:480
  128.4 2.4 %all-gather.6 = bf16[256,1536]{1,0:T(8,128)(2,1)S(1)} all-gather(bf16[128,1536]{1,0:T(8,128)(2,1)S(1)} %get-tuple-element.40), channel_id=8, replica_groups={{0,8},{16,24},{1,9},{17,25},{2,10},{18,26},{3,11},{19,27},{4,12},{20,28..., dimensions={0}, use_global_device_ids=true | all-gather | bytes 1179648 | tf_op jit(solution)/shard_map/all_gather | solution.py:356
  130.8 0.6 finish2.1
  131.4 1.9 %collective-permute-start.10 = (bf16[64,1536]{1,0:T(8,128)(2,1)S(1)}, bf16[64,1536]{1,0:T(8,128)(2,1)S(1)}, u32[]{:S(2)}, u32[]{:S(2)}) collective-permute-start(bf16[64,1536]{1,0:T(8,128)(2,1)S(1)} %get-tuple-element.45), channel_id=1, source_target_pairs={{0,5},{1,4},{2,7},{3,6},{4,1},{5,0},{6,3},{7,2},{8,13},{9,12},{10,... | collective-permute-start | bytes 589832 | tf_op jit(solution)/shard_map/ppermute | solution.py:514
  133.3 2.7 %collective-permute-start.9 = (bf16[64,1536]{1,0:T(8,128)(2,1)S(1)}, bf16[64,1536]{1,0:T(8,128)(2,1)S(1)}, u32[]{:S(2)}, u32[]{:S(2)}) collective-permute-start(bf16[64,1536]{1,0:T(8,128)(2,1)S(1)} %get-tuple-element.41.refs_4_), channel_id=1, source_target_pairs={{0,4},{1,5},{2,6},{3,7},{4,0},{5,1},{6,2},{7,3},{8,12},{9,13},{10,... | collective-permute-start | bytes 589832 | tf_op jit(solution)/shard_map/ppermute | solution.py:514
  135.9 3.5 %collective-permute-done.7.refs_1_ = bf16[128,4096]{1,0:T(8,128)(2,1)} collective-permute-done((bf16[128,4096]{1,0:T(8,128)(2,1)}, bf16[128,4096]{1,0:T(8,128)(2,1)}, u32[]{:S(2)}, u32[]{:S(2)}) %collective-permute-start.7) | collective-permute-done | bytes 1048608 | tf_op jit(solution)/shard_map/ppermute | solution.py:459
  139.4 10.7 %down3_0.1 = (f32[128,1536]{1,0:T(8,128)S(1)}, bf16[128,1536]{1,0:T(8,128)(2,1)S(1)}) custom-call(s32[2]{0:T(128)S(1)} %copy-done.8, bf16[128,4096]{1,0:T(8,128)(2,1)} %get-tuple-element.34.t_ref.refs_0_, bf16[128,4096]{1,0:T(8,128)(2,1)} %collective-permute-done.7.refs_1_, bf16[8192,1536]{1,0:T(8,128)(2,1)} %refs_2_.5, ...), custom_call_target="tpu_custom_call" | custom-call | flops 1 | bytes 1 | tf_op jit(solution)/shard_map/down3_0/pallas_call | solution.py:480
  150.1 2.4 %all-gather.7 = bf16[256,1536]{1,0:T(8,128)(2,1)S(1)} all-gather(bf16[128,1536]{1,0:T(8,128)(2,1)S(1)} %get-tuple-element.43), channel_id=9, replica_groups={{0,8},{16,24},{1,9},{17,25},{2,10},{18,26},{3,11},{19,27},{4,12},{20,28..., dimensions={0}, use_global_device_ids=true | all-gather | bytes 1179648 | tf_op jit(solution)/shard_map/all_gather | solution.py:356
  152.4 0.6 finish3.1
  153.0 1.9 %collective-permute-start.12 = (bf16[64,1536]{1,0:T(8,128)(2,1)S(1)}, bf16[64,1536]{1,0:T(8,128)(2,1)S(1)}, u32[]{:S(2)}, u32[]{:S(2)}) collective-permute-start(bf16[64,1536]{1,0:T(8,128)(2,1)S(1)} %get-tuple-element.46), channel_id=1, source_target_pairs={{0,7},{1,6},{2,5},{3,4},{4,3},{5,2},{6,1},{7,0},{8,15},{9,14},{10,... | collective-permute-start | bytes 589832 | tf_op jit(solution)/shard_map/ppermute | solution.py:514
  154.9 1.7 collective-permute-start.11
  156.6 0.0 all-to-all-done.2.refs_0_
  156.6 1.4 combine1.1.acc_ref.refs_2_
  158.0 0.0 collective-permute-done.10.refs_1_
  158.1 0.0 collective-permute-done.9.refs_0_
  158.1 1.4 combine2.1.acc_ref.refs_2_
  159.4 10.8 %collective-permute-done.12.refs_1_ = bf16[64,1536]{1,0:T(8,128)(2,1)S(1)} collective-permute-done((bf16[64,1536]{1,0:T(8,128)(2,1)S(1)}, bf16[64,1536]{1,0:T(8,128)(2,1)S(1)}, u32[]{:S(2)}, u32[]{:S(2)}) %collective-permute-start.12) | collective-permute-done | bytes 196640 | tf_op jit(solution)/shard_map/ppermute | solution.py:514
  170.2 4.0 %collective-permute-done.11.refs_0_ = bf16[64,1536]{1,0:T(8,128)(2,1)S(1)} collective-permute-done((bf16[64,1536]{1,0:T(8,128)(2,1)S(1)}, bf16[64,1536]{1,0:T(8,128)(2,1)S(1)}, u32[]{:S(2)}, u32[]{:S(2)}) %collective-permute-start.11) | collective-permute-done | bytes 196640 | tf_op jit(solution)/shard_map/ppermute | solution.py:514
  174.2 2.3 %combine3.1 = bf16[256,1536]{1,0:T(8,128)(2,1)} custom-call(s32[2]{0:T(128)S(1)} %copy-done.8, s32[2,256]{1,0:T(2,128)S(1)} %bitcast.25, f32[8,256]{1,0:T(8,128)S(1)} %copy-done.5, f32[8,256]{1,0:T(8,128)S(1)} %copy-done.3, f32[256,1536]{1,0:T(8,128)S(1)} %combine2.1.acc_ref.refs_2_, bf16[64,1536]{1,0:T(8,128)(2,1)S(1)} %collective-permute-done.11.refs_0_, ...), custom_call_target="tpu_custom_call" | custom-call | flops 1 | bytes 1 | tf_op jit(solution)/shard_map/combine3/pallas_call | solution.py:520
  (23 shorter events, 0.0 us)
Async XLA Ops:
  0.0 1.1 copy-start
  1.1 0.7 copy-start.9
  1.8 0.7 copy-start.11
  5.3 12.6 %copy-start.4 = (f32[8,256]{1,0:T(8,128)}, f32[8,256]{1,0:T(8,128)S(1)}, u32[]{:S(2)}) copy-start(f32[8,256]{1,0:T(8,128)S(1)} %get-tuple-element.26.t_ref.slot_ref) | copy-start | bytes 24580
  5.3 19.4 %all-to-all-start = ((bf16[4,64,1536]{2,1,0:T(8,128)(2,1)}), bf16[4,64,1536]{2,1,0:T(8,128)(2,1)S(1)}, u32[]{:S(2)}, u32[]{:S(2)}) async-start(bf16[4,64,1536]{2,1,0:T(8,128)(2,1)} %get-tuple-element.28), calls=%async_computation | async-start | bytes 1572864 | tf_op jit(solution)/shard_map/all_to_all | solution.py:359
  9.0 1.2 collective-permute-start
  10.2 14.4 %collective-permute-start.1 = (f32[8,256]{1,0:T(8,128)S(1)}, f32[8,256]{1,0:T(8,128)S(1)}, u32[]{:S(2)}, u32[]{:S(2)}) collective-permute-start(f32[8,256]{1,0:T(8,128)S(1)} %add.11), channel_id=1, source_target_pairs={{0,16},{8,24},{16,0},{24,8},{1,17},{9,25},{17,1},{25,9},{2,18},{10... | collective-permute-start | bytes 24584 | tf_op jit(solution)/shard_map/ppermute | solution.py:378
  11.8 6.2 %copy-start.6 = (s32[2]{0:T(128)}, s32[2]{0:T(128)S(1)}, u32[]{:S(2)}) copy-start(s32[2]{0:T(128)S(1)} %pad_add_fusion.me_ref) | copy-start | bytes 28
  17.9 22.1 %collective-permute-start.2 = (bf16[2048,1536]{1,0:T(8,128)(2,1)}, bf16[2048,1536]{1,0:T(8,128)(2,1)}, u32[]{:S(2)}, u32[]{:S(2)}) collective-permute-start(bf16[2048,1536]{1,0:T(8,128)(2,1)} %cut0.1.t_ref), channel_id=1, source_target_pairs={{0,8},{8,0},{16,24},{24,16},{1,9},{9,1},{17,25},{25,17},{2,10},{10... | collective-permute-start | bytes 18874376 | tf_op jit(solution)/shard_map/ppermute | solution.py:353
  24.1 33.2 %collective-permute-start.4 = (bf16[2048,1536]{1,0:T(8,128)(2,1)}, bf16[2048,1536]{1,0:T(8,128)(2,1)}, u32[]{:S(2)}, u32[]{:S(2)}) collective-permute-start(bf16[2048,1536]{1,0:T(8,128)(2,1)} %cut1.1.t_ref), channel_id=1, source_target_pairs={{0,8},{8,0},{16,24},{24,16},{1,9},{9,1},{17,25},{25,17},{2,10},{10... | collective-permute-start | bytes 18874376 | tf_op jit(solution)/shard_map/ppermute | solution.py:353
  24.6 54.9 %copy-start.2 = (f32[8,256]{1,0:T(8,128)}, f32[8,256]{1,0:T(8,128)S(1)}, u32[]{:S(2)}) copy-start(f32[8,256]{1,0:T(8,128)S(1)} %add.12.refs_8_.logit_ref) | copy-start | bytes 24580
  24.6 41.7 %all-to-all-start.1 = ((bf16[8,64,1536]{2,1,0:T(8,128)(2,1)}), bf16[8,64,1536]{2,1,0:T(8,128)(2,1)}, u32[]{:S(2)}, u32[]{:S(2)}) async-start(bf16[8,64,1536]{2,1,0:T(8,128)(2,1)} %get-tuple-element.31), calls=%async_computation.1 | async-start | bytes 3145728 | tf_op jit(solution)/shard_map/all_to_all | solution.py:374
  31.2 8.9 %copy-start.7 = (s32[2]{0:T(128)S(1)}, s32[2]{0:T(128)}, u32[]{:S(2)}) copy-start(s32[2]{0:T(128)} %copy-done.6) | copy-start | bytes 28
  46.6 46.8 %collective-permute-start.3 = (bf16[256,2048]{1,0:T(8,128)(2,1)S(1)}, bf16[256,2048]{1,0:T(8,128)(2,1)S(1)}, u32[]{:S(2)}, u32[]{:S(2)}) collective-permute-start(bf16[256,2048]{1,0:T(8,128)(2,1)S(1)} %up1_0.1.t_ref.a_ref), channel_id=1, source_target_pairs={{0,16},{8,24},{16,0},{24,8},{1,17},{9,25},{17,1},{25,9},{2,18},{10... | collective-permute-start | bytes 3145736 | tf_op jit(solution)/shard_map/ppermute | solution.py:459
  57.1 39.5 %collective-permute-start.6 = (bf16[4096,1536]{1,0:T(8,128)(2,1)}, bf16[4096,1536]{1,0:T(8,128)(2,1)}, u32[]{:S(2)}, u32[]{:S(2)}) collective-permute-start(bf16[4096,1536]{1,0:T(8,128)(2,1)} %cutNone.1.refs_7_), channel_id=1, source_target_pairs={{0,8},{8,0},{16,24},{24,16},{1,9},{9,1},{17,25},{25,17},{2,10},{10... | collective-permute-start | bytes 37748744 | tf_op jit(solution)/shard_map/ppermute | solution.py:353
  64.8 29.7 %collective-permute-start.5 = (bf16[256,2048]{1,0:T(8,128)(2,1)}, bf16[256,2048]{1,0:T(8,128)(2,1)}, u32[]{:S(2)}, u32[]{:S(2)}) collective-permute-start(bf16[256,2048]{1,0:T(8,128)(2,1)} %up1_2.1.t_ref.a_ref), channel_id=1, source_target_pairs={{0,16},{8,24},{16,0},{24,8},{1,17},{9,25},{17,1},{25,9},{2,18},{10... | collective-permute-start | bytes 3145736 | tf_op jit(solution)/shard_map/ppermute | solution.py:459
  91.3 26.4 %collective-permute-start.8 = (bf16[128,4096]{1,0:T(8,128)(2,1)}, bf16[128,4096]{1,0:T(8,128)(2,1)}, u32[]{:S(2)}, u32[]{:S(2)}) collective-permute-start(bf16[128,4096]{1,0:T(8,128)(2,1)} %get-tuple-element.38.refs_0_), channel_id=1, source_target_pairs={{0,16},{8,24},{16,0},{24,8},{1,17},{9,25},{17,1},{25,9},{2,18},{10... | collective-permute-start | bytes 3145736 | tf_op jit(solution)/shard_map/ppermute | solution.py:459
  92.9 46.4 %collective-permute-start.7 = (bf16[128,4096]{1,0:T(8,128)(2,1)}, bf16[128,4096]{1,0:T(8,128)(2,1)}, u32[]{:S(2)}, u32[]{:S(2)}) collective-permute-start(bf16[128,4096]{1,0:T(8,128)(2,1)} %get-tuple-element.34.t_ref.refs_0_), channel_id=1, source_target_pairs={{0,16},{8,24},{16,0},{24,8},{1,17},{9,25},{17,1},{25,9},{2,18},{10... | collective-permute-start | bytes 3145736 | tf_op jit(solution)/shard_map/ppermute | solution.py:459
  113.6 43.0 %all-to-all-start.2 = ((bf16[4,64,1536]{2,1,0:T(8,128)(2,1)}), bf16[4,64,1536]{2,1,0:T(8,128)(2,1)S(1)}, u32[]{:S(2)}, u32[]{:S(2)}) async-start(bf16[4,64,1536]{2,1,0:T(8,128)(2,1)} %finish1.1.refs_4_), calls=%async_computation.2 | async-start | bytes 1572864 | tf_op jit(solution)/shard_map/all_to_all | solution.py:359
  117.8 21.6 %copy-start.8 = (s32[2]{0:T(128)S(1)}, s32[2]{0:T(128)}, u32[]{:S(2)}) copy-start(s32[2]{0:T(128)} %copy-done.6) | copy-start | bytes 28
  131.4 26.6 %collective-permute-start.10 = (bf16[64,1536]{1,0:T(8,128)(2,1)S(1)}, bf16[64,1536]{1,0:T(8,128)(2,1)S(1)}, u32[]{:S(2)}, u32[]{:S(2)}) collective-permute-start(bf16[64,1536]{1,0:T(8,128)(2,1)S(1)} %get-tuple-element.45), channel_id=1, source_target_pairs={{0,5},{1,4},{2,7},{3,6},{4,1},{5,0},{6,3},{7,2},{8,13},{9,12},{10,... | collective-permute-start | bytes 589832 | tf_op jit(solution)/shard_map/ppermute | solution.py:514
  133.3 23.3 %copy-start.1 = (bf16[256,1536]{1,0:T(8,128)(2,1)S(1)}, bf16[256,1536]{1,0:T(8,128)(2,1)}, u32[]{:S(2)}) copy-start(bf16[256,1536]{1,0:T(8,128)(2,1)} %acc_ref.1) | copy-start | bytes 2359300
  133.3 23.3 %copy-start.3 = (f32[8,256]{1,0:T(8,128)S(1)}, f32[8,256]{1,0:T(8,128)}, u32[]{:S(2)}) copy-start(f32[8,256]{1,0:T(8,128)} %copy-done.2) | copy-start | bytes 24580
  133.3 23.3 %copy-start.5 = (f32[8,256]{1,0:T(8,128)S(1)}, f32[8,256]{1,0:T(8,128)}, u32[]{:S(2)}) copy-start(f32[8,256]{1,0:T(8,128)} %copy-done.4) | copy-start | bytes 24580
  133.3 23.4 %copy-start.10 = (s32[256,2]{0,1:T(2,128)S(1)}, s32[256,2]{0,1:T(2,128)}, u32[]{:S(2)}) copy-start(s32[256,2]{0,1:T(2,128)} %param.9) | copy-start | bytes 6148
  133.3 24.8 %collective-permute-start.9 = (bf16[64,1536]{1,0:T(8,128)(2,1)S(1)}, bf16[64,1536]{1,0:T(8,128)(2,1)S(1)}, u32[]{:S(2)}, u32[]{:S(2)}) collective-permute-start(bf16[64,1536]{1,0:T(8,128)(2,1)S(1)} %get-tuple-element.41.refs_4_), channel_id=1, source_target_pairs={{0,4},{1,5},{2,6},{3,7},{4,0},{5,1},{6,2},{7,3},{8,12},{9,13},{10,... | collective-permute-start | bytes 589832 | tf_op jit(solution)/shard_map/ppermute | solution.py:514
  153.0 17.1 %collective-permute-start.12 = (bf16[64,1536]{1,0:T(8,128)(2,1)S(1)}, bf16[64,1536]{1,0:T(8,128)(2,1)S(1)}, u32[]{:S(2)}, u32[]{:S(2)}) collective-permute-start(bf16[64,1536]{1,0:T(8,128)(2,1)S(1)} %get-tuple-element.46), channel_id=1, source_target_pairs={{0,7},{1,6},{2,5},{3,4},{4,3},{5,2},{6,1},{7,0},{8,15},{9,14},{10,... | collective-permute-start | bytes 589832 | tf_op jit(solution)/shard_map/ppermute | solution.py:514
  154.9 19.2 %collective-permute-start.11 = (bf16[64,1536]{1,0:T(8,128)(2,1)S(1)}, bf16[64,1536]{1,0:T(8,128)(2,1)S(1)}, u32[]{:S(2)}, u32[]{:S(2)}) collective-permute-start(bf16[64,1536]{1,0:T(8,128)(2,1)S(1)} %get-tuple-element.44.refs_1_), channel_id=1, source_target_pairs={{0,6},{1,7},{2,4},{3,5},{4,2},{5,3},{6,0},{7,1},{8,14},{9,15},{10,... | collective-permute-start | bytes 589832 | tf_op jit(solution)/shard_map/ppermute | solution.py:514

commit v2 on v1

--- a/solution.py
+++ b/solution.py
@@ -219,12 +219,10 @@
     stream([(locate_a, buf_a, sem_a), (locate_b, buf_b, sem_b)], each * n_p, use)
 
 
-def down_kernel(half, plan, ready, has_acc, me_ref, *refs):
-    n_in = plan[-1][1] + 1
-    wide = 1 if ready else 2
-    s_refs = refs[: wide * n_in]
-    w_ref, got_ref = refs[wide * n_in : wide * n_in + 2]
-    k = wide * n_in + 2
+def down_kernel(half, plan, n_in, has_acc, me_ref, *refs):
+    s_refs = refs[:n_in]
+    w_ref, got_ref = refs[n_in : n_in + 2]
+    k = n_in + 2
     acc_refs = refs[k : k + 2] if has_acc else None
     k += 1 + (2 if has_acc else 0)
     own_ref, *oth_refs = refs[k:-7]
@@ -238,12 +236,12 @@
         return got_ref, plan[g][0]
 
     def use(g, a, b):
-        _, i, c = plan[g]
+        _, which, c = plan[g]
         cols = slice(c, c + TILE)
-        if ready:
-            h[...] = s_refs[i][:, cols]
+        if len(which) == 1:
+            h[...] = s_refs[which[0]][:, cols]
         else:
-            v = s_refs[2 * i][:, cols].astype(F32) + s_refs[2 * i + 1][:, cols].astype(F32)
+            v = s_refs[which[0]][:, cols].astype(F32) + s_refs[which[1]][:, cols].astype(F32)
             h[...] = (v / (1.0 + jnp.exp(-v))).astype(BF)
         for i, (total, w) in enumerate(((own, a), (oth, b))):
             part = jnp.dot(h[...], w[...], preferred_element_type=F32)
@@ -309,7 +307,7 @@
     out_ref[...] = total.astype(out_ref.dtype)
 
 
-CHUNKS = ((), (0, 1, 2, 3), (4, 5), (6, 7))
+CHUNKS = ((), (0, 1, 2, 3), (6, 7), (4, 5))
 ORDER = (
     ("W", 0),
     ("W", 1),
@@ -320,7 +318,6 @@
     ("X", (2, 3)),
     ("U", (2, 3), (0, 1, 2, 3), ((3, (0, 1, 2, 3)), (2, (0, 1, 2, 3)))),
     ("H", 1, (0, 1)),
-    ("H", 1, (2, 3)),
     ("D", 1, (0, 1, 2, 3)),
     ("F", 1),
     ("D", 2, (0, 1, 2, 3)),
@@ -462,23 +459,19 @@
 
     def down(c, pieces, final):
         nonlocal tok
-        held = [p for p in pieces if not isinstance(sums[c, p][0], tuple)]
-        if held and len(held) < len(pieces):
-            down(c, held, False)
-            pieces = [p for p in pieces if p not in held]
-        ready = not isinstance(sums[c, pieces[0]][0], tuple)
-        arrays, plan = [], []
+        flat, plan, last = [], [], None
         for p in pieces:
             pair, at = sums[c, p]
-            if not arrays or arrays[-1] is not pair:
-                arrays.append(pair)
-            plan += [(p * span + t, len(arrays) - 1, at + t) for t in range(0, span, TILE)]
-        flat = arrays if ready else [v for pair in arrays for v in pair]
+            if pair is not last:
+                last, found = pair, pair if isinstance(pair, tuple) else (pair,)
+                which = range(len(flat), len(flat) + len(found))
+                flat += found
+            plan += [(p * span + t, which, at + t) for t in range(0, span, TILE)]
         n = cap * len(CHUNKS[c])
         acc = partial.get(c, ())
         parts = 2 if final and c == 1 else 1
         res = kernel_call(
-            functools.partial(down_kernel, half, plan, ready, len(acc) > 0),
+            functools.partial(down_kernel, half, plan, len(flat), len(acc) > 0),
             out_shape=[sds((n, columns), F32)] + [sds((n // parts, columns), BF if final else F32)] * parts,
             in_specs=[SM] + [VM] * len(flat) + [HBM, ANY] + [VM] * len(acc) + [ANY],
             out_specs=[VM] * (1 + parts),

time: 177 us -> 179 us (1.011)
  the two profiles are of different devices: /device:TPU:16 before, /device:TPU:0 now
where the time goes in v2:
time: 179 us
  Pallas kernels  93.6 us (52%)
  starting transfers between devices  32 us (18%)
  blocking collectives  28.4 us (16%)
  waiting for transfers between devices  22 us (12%)
  local copies, waits for them, and re-layouts  2.58 us (1%)
    pallas_call x3, Pallas kernels, down(): kernel_call(functools.partial(down_kernel, half, plan, len(flat), len(acc...  32.9 us
    all_gather x8, blocking collectives, core_pair(): return lax.all_gather(v, 'section', axis_index_groups=[[0, 1], [2, 3]])  28.4 us
    pallas_call x3, Pallas kernels, up(): kernel_call(functools.partial(up_kernel, half, span, pieces, len(mine), c...  26 us
    pallas_call x3, Pallas kernels, cut(): kernel_call(functools.partial(cut_kernel, i * rows if i else 0, half), ou...  22.1 us
    ppermute x4, waiting for transfers between devices, finish(): lax.ppermute(r, 'expert', peer(j))  14.7 us
    ppermute x4, starting transfers between devices, finish(): lax.ppermute(r, 'expert', peer(j))  9.86 us
    all_to_all x2, starting transfers between devices, near_swap(): lax.all_to_all(v, 'expert', split_axis=0, concat_axis=0, axis_index_group...  9.41 us
    all_to_all x1, starting transfers between devices, pipelined(): lax.all_to_all(all_rows, 'expert', split_axis=0, concat_axis=0, tiled=True)  6.24 us
  transfers between devices with their start and end apart: 16, of which 7 were waited for; matrix products, arithmetic and copies ran while one was open for 0% of the time, Pallas kernels for 50%

profile of v2, /device:TPU:0, one launch (start us, length us, event | category | flops | bytes accessed | tf_op | source)
XLA Modules:
  0.0 178.8 jit_solution(15173351713751131295)
XLA Ops:
  0.0 1.1 copy-done
  1.1 0.7 copy-done.9
  1.8 0.7 copy-done.11
  2.6 2.7 %route.1 = (f32[8,256]{1,0:T(8,128)S(1)}, f32[8,256]{1,0:T(8,128)S(1)}, bf16[4,64,1536]{2,1,0:T(8,128)(2,1)}, bf16[8,64,1536]{2,1,0:T(8,128)(2,1)}) custom-call(s32[1]{0:T(128)} %bitcast.3.me_ref, s32[2,256]{1,0:T(2,128)S(1)} %bitcast.22, bf16[256,1536]{1,0:T(8,128)(2,1)S(1)} %copy-done, bf16[8,1536]{1,0:T(8,128)(2,1)S(1)} %copy-done.11), custom_call_target="tpu_custom_call" | custom-call | flops 1 | bytes 1 | tf_op jit(solution)/shard_map/route/pallas_call | solution.py:361
  5.3 5.2 %all-to-all-start = ((bf16[4,64,1536]{2,1,0:T(8,128)(2,1)}), bf16[4,64,1536]{2,1,0:T(8,128)(2,1)S(1)}, u32[]{:S(2)}, u32[]{:S(2)}) async-start(bf16[4,64,1536]{2,1,0:T(8,128)(2,1)} %get-tuple-element.28), calls=%async_computation | async-start | bytes 1572864 | tf_op jit(solution)/shard_map/all_to_all | solution.py:356
  10.5 0.0 collective-permute-start
  10.5 1.2 collective-permute-done
  11.7 1.5 collective-permute-start.1
  13.2 0.1 pad_add_fusion.me_ref
  13.3 6.1 %cut0.1.t_ref = bf16[2048,1536]{1,0:T(8,128)(2,1)} custom-call(s32[2]{0:T(128)S(1)} %pad_add_fusion.me_ref, bf16[8192,1536]{1,0:T(8,128)(2,1)} %refs_4_.5, f32[8,256]{1,0:T(8,128)S(1)} %get-tuple-element.26.t_ref.slot_ref), custom_call_target="tpu_custom_call" | custom-call | flops 1 | bytes 1 | tf_op jit(solution)/shard_map/cut0/pallas_call | solution.py:381
  19.3 0.1 collective-permute-start.2
  19.4 6.1 %cut1.1.t_ref = bf16[2048,1536]{1,0:T(8,128)(2,1)} custom-call(s32[2]{0:T(128)S(1)} %pad_add_fusion.me_ref, bf16[8192,1536]{1,0:T(8,128)(2,1)} %refs_4_.5, bf16[2048,1536]{1,0:T(8,128)(2,1)} %cut0.1.t_ref), custom_call_target="tpu_custom_call" | custom-call | flops 1 | bytes 1 | tf_op jit(solution)/shard_map/cut1/pallas_call | solution.py:381
  25.5 0.6 collective-permute-start.4
  26.1 0.0 collective-permute-done.1
  26.1 0.0 all-to-all-done.a_ref
  26.1 6.2 %all-to-all-start.1 = ((bf16[8,64,1536]{2,1,0:T(8,128)(2,1)}), bf16[8,64,1536]{2,1,0:T(8,128)(2,1)}, u32[]{:S(2)}, u32[]{:S(2)}) async-start(bf16[8,64,1536]{2,1,0:T(8,128)(2,1)} %get-tuple-element.31), calls=%async_computation.1 | async-start | bytes 3145728 | tf_op jit(solution)/shard_map/all_to_all | solution.py:371
  32.3 0.1 pack1.1
  32.4 6.8 %all-gather = bf16[256,1536]{1,0:T(8,128)(2,1)S(1)} all-gather(bf16[128,1536]{1,0:T(8,128)(2,1)S(1)} %get-tuple-element.29.refs_0_.refs_7_), channel_id=2, replica_groups={{0,8},{16,24},{1,9},{17,25},{2,10},{18,26},{3,11},{19,27},{4,12},{20,28..., dimensions={0}, use_global_device_ids=true | all-gather | bytes 1179648 | tf_op jit(solution)/shard_map/all_gather | solution.py:353
  39.1 2.4 %all-gather.1 = bf16[256,1536]{1,0:T(8,128)(2,1)S(1)} all-gather(bf16[128,1536]{1,0:T(8,128)(2,1)S(1)} %get-tuple-element.30.refs_1_), channel_id=3, replica_groups={{0,8},{16,24},{1,9},{17,25},{2,10},{18,26},{3,11},{19,27},{4,12},{20,28..., dimensions={0}, use_global_device_ids=true | all-gather | bytes 1179648 | tf_op jit(solution)/shard_map/all_gather | solution.py:353
  41.5 0.0 collective-permute-done.2.refs_5_.refs_6_
  41.5 6.5 %up1_0.1.t_ref.a_ref = bf16[256,2048]{1,0:T(8,128)(2,1)S(1)} custom-call(s32[2]{0:T(128)S(1)} %copy-done.7, bf16[128,1536]{1,0:T(8,128)(2,1)S(1)} %get-tuple-element.29.refs_0_.refs_7_, bf16[128,1536]{1,0:T(8,128)(2,1)S(1)} %get-tuple-element.30.refs_1_, bf16[2,128,1536]{2,1,0:T(8,128)(2,1)S(1)} %bitcast.12, bf16[2,128,1536]{2,1,0:T(8,128)(2,1)S(1)} %bitcast.14, ...), custom_call_target="tpu_custom_call" | custom-call | flops 1 | bytes 1 | tf_op jit(solution)/shard_map/up1_0/pallas_call | solution.py:444
  48.0 0.6 collective-permute-start.3
  48.6 10.0 %cutNone.1.refs_7_ = bf16[4096,1536]{1,0:T(8,128)(2,1)} custom-call(s32[2]{0:T(128)S(1)} %copy-done.7, bf16[8192,1536]{1,0:T(8,128)(2,1)} %refs_2_.3, bf16[256,2048]{1,0:T(8,128)(2,1)S(1)} %up1_0.1.t_ref.a_ref), custom_call_target="tpu_custom_call" | custom-call | flops 1 | bytes 1 | tf_op jit(solution)/shard_map/cutNone/pallas_call | solution.py:381
  58.6 0.1 collective-permute-start.6
  58.7 0.0 collective-permute-done.4.refs_6_
  58.7 7.5 %up1_2.1.t_ref.refs_1_ = bf16[256,2048]{1,0:T(8,128)(2,1)} custom-call(s32[2]{0:T(128)S(1)} %copy-done.7, bf16[128,1536]{1,0:T(8,128)(2,1)S(1)} %get-tuple-element.29.refs_0_.refs_7_, bf16[128,1536]{1,0:T(8,128)(2,1)S(1)} %get-tuple-element.30.refs_1_, bf16[2,128,1536]{2,1,0:T(8,128)(2,1)S(1)} %bitcast.13, bf16[2,128,1536]{2,1,0:T(8,128)(2,1)S(1)} %bitcast.15, ...), custom_call_target="tpu_custom_call" | custom-call | flops 1 | bytes 1 | tf_op jit(solution)/shard_map/up1_2/pallas_call | solution.py:444
  66.2 1.6 collective-permute-start.5
  67.8 1.8 %all-to-all-done.1.a_ref = bf16[8,64,1536]{2,1,0:T(8,128)(2,1)} async-done(((bf16[8,64,1536]{2,1,0:T(8,128)(2,1)}), bf16[8,64,1536]{2,1,0:T(8,128)(2,1)}, u32[]{:S(2)}, u32[]{:S(2)}) %all-to-all-start.1) | async-done | bytes 1572896 | tf_op jit(solution)/shard_map/all_to_all | solution.py:371
  69.6 1.5 pack2.1
  71.1 7.3 %all-gather.2 = bf16[256,1536]{1,0:T(8,128)(2,1)S(1)} all-gather(bf16[128,1536]{1,0:T(8,128)(2,1)S(1)} %get-tuple-element.32.refs_0_.refs_7_), channel_id=4, replica_groups={{0,8},{16,24},{1,9},{17,25},{2,10},{18,26},{3,11},{19,27},{4,12},{20,28..., dimensions={0}, use_global_device_ids=true | all-gather | bytes 1179648 | tf_op jit(solution)/shard_map/all_gather | solution.py:353
  78.4 2.5 %all-gather.3 = bf16[256,1536]{1,0:T(8,128)(2,1)S(1)} all-gather(bf16[128,1536]{1,0:T(8,128)(2,1)S(1)} %get-tuple-element.33.refs_1_), channel_id=5, replica_groups={{0,8},{16,24},{1,9},{17,25},{2,10},{18,26},{3,11},{19,27},{4,12},{20,28..., dimensions={0}, use_global_device_ids=true | all-gather | bytes 1179648 | tf_op jit(solution)/shard_map/all_gather | solution.py:353
  80.9 0.0 copy-done.2
  80.9 11.9 %up23_0.1 = (bf16[128,4096]{1,0:T(8,128)(2,1)}, bf16[128,4096]{1,0:T(8,128)(2,1)}) custom-call(s32[2]{0:T(128)S(1)} %copy-done.7, bf16[128,1536]{1,0:T(8,128)(2,1)S(1)} %get-tuple-element.32.refs_0_.refs_7_, bf16[128,1536]{1,0:T(8,128)(2,1)S(1)} %get-tuple-element.33.refs_1_, bf16[2,128,1536]{2,1,0:T(8,128)(2,1)S(1)} %bitcast.20, ...), custom_call_target="tpu_custom_call" | custom-call | flops 1 | bytes 1 | tf_op jit(solution)/shard_map/up23_0/pallas_call | solution.py:444
  92.8 1.6 collective-permute-start.8
  94.4 0.5 collective-permute-start.7
  94.9 0.0 collective-permute-done.3.b_ref
  94.9 0.7 silu1.1.refs_0_.refs_5_
  95.6 0.3 collective-permute-done.5.refs_2_
  95.9 0.0 collective-permute-done.6.refs_4_.refs_3_
  95.9 11.6 %down1_0.1 = (f32[256,1536]{1,0:T(8,128)S(1)}, bf16[128,1536]{1,0:T(8,128)(2,1)S(1)}, bf16[128,1536]{1,0:T(8,128)(2,1)S(1)}) custom-call(s32[2]{0:T(128)S(1)} %copy-done.7, bf16[256,2048]{1,0:T(8,128)(2,1)S(1)} %silu1.1.refs_0_.refs_5_, bf16[256,2048]{1,0:T(8,128)(2,1)} %up1_2.1.t_ref.refs_1_, bf16[256,2048]{1,0:T(8,128)(2,1)} %collective-permute-done.5.refs_2_, ...), custom_call_target="tpu_custom_call" | custom-call | flops 1 | bytes 1 | tf_op jit(solution)/shard_map/down1_0/pallas_call | solution.py:473
  107.5 2.4 %all-gather.4 = bf16[256,1536]{1,0:T(8,128)(2,1)S(1)} all-gather(bf16[128,1536]{1,0:T(8,128)(2,1)S(1)} %get-tuple-element.36), channel_id=6, replica_groups={{0,8},{16,24},{1,9},{17,25},{2,10},{18,26},{3,11},{19,27},{4,12},{20,28..., dimensions={0}, use_global_device_ids=true | all-gather | bytes 1179648 | tf_op jit(solution)/shard_map/all_gather | solution.py:353
  109.8 2.4 %all-gather.5 = bf16[256,1536]{1,0:T(8,128)(2,1)S(1)} all-gather(bf16[128,1536]{1,0:T(8,128)(2,1)S(1)} %get-tuple-element.37), channel_id=7, replica_groups={{0,8},{16,24},{1,9},{17,25},{2,10},{18,26},{3,11},{19,27},{4,12},{20,28..., dimensions={0}, use_global_device_ids=true | all-gather | bytes 1179648 | tf_op jit(solution)/shard_map/all_gather | solution.py:353
  112.2 1.6 finish1.1.refs_4_
  113.7 4.2 %all-to-all-start.2 = ((bf16[4,64,1536]{2,1,0:T(8,128)(2,1)}), bf16[4,64,1536]{2,1,0:T(8,128)(2,1)S(1)}, u32[]{:S(2)}, u32[]{:S(2)}) async-start(bf16[4,64,1536]{2,1,0:T(8,128)(2,1)} %finish1.1.refs_4_), calls=%async_computation.2 | async-start | bytes 1572864 | tf_op jit(solution)/shard_map/all_to_all | solution.py:356
  117.9 1.3 collective-permute-done.8.refs_1_
  119.2 10.6 %down2_0.1 = (f32[128,1536]{1,0:T(8,128)S(1)}, bf16[128,1536]{1,0:T(8,128)(2,1)S(1)}) custom-call(s32[2]{0:T(128)S(1)} %copy-done.7, bf16[128,4096]{1,0:T(8,128)(2,1)} %get-tuple-element.38.refs_0_, bf16[128,4096]{1,0:T(8,128)(2,1)} %collective-permute-done.8.refs_1_, bf16[8192,1536]{1,0:T(8,128)(2,1)} %refs_2_.3, ...), custom_call_target="tpu_custom_call" | custom-call | flops 1 | bytes 1 | tf_op jit(solution)/shard_map/down2_0/pallas_call | solution.py:473
  129.9 2.4 %all-gather.6 = bf16[256,1536]{1,0:T(8,128)(2,1)S(1)} all-gather(bf16[128,1536]{1,0:T(8,128)(2,1)S(1)} %get-tuple-element.40), channel_id=8, replica_groups={{0,8},{16,24},{1,9},{17,25},{2,10},{18,26},{3,11},{19,27},{4,12},{20,28..., dimensions={0}, use_global_device_ids=true | all-gather | bytes 1179648 | tf_op jit(solution)/shard_map/all_gather | solution.py:353
  132.2 0.6 finish2.1
  132.9 5.0 %collective-permute-start.10 = (bf16[64,1536]{1,0:T(8,128)(2,1)S(1)}, bf16[64,1536]{1,0:T(8,128)(2,1)S(1)}, u32[]{:S(2)}, u32[]{:S(2)}) collective-permute-start(bf16[64,1536]{1,0:T(8,128)(2,1)S(1)} %get-tuple-element.45), channel_id=1, source_target_pairs={{0,7},{1,6},{2,5},{3,4},{4,3},{5,2},{6,1},{7,0},{8,15},{9,14},{10,... | collective-permute-start | bytes 589832 | tf_op jit(solution)/shard_map/ppermute | solution.py:507
  137.9 0.4 collective-permute-start.9
  138.3 2.6 %collective-permute-done.7.refs_1_ = bf16[128,4096]{1,0:T(8,128)(2,1)} collective-permute-done((bf16[128,4096]{1,0:T(8,128)(2,1)}, bf16[128,4096]{1,0:T(8,128)(2,1)}, u32[]{:S(2)}, u32[]{:S(2)}) %collective-permute-start.7) | collective-permute-done | bytes 1048608 | tf_op jit(solution)/shard_map/ppermute | solution.py:456
  140.9 10.6 %down3_0.1 = (f32[128,1536]{1,0:T(8,128)S(1)}, bf16[128,1536]{1,0:T(8,128)(2,1)S(1)}) custom-call(s32[2]{0:T(128)S(1)} %copy-done.8, bf16[128,4096]{1,0:T(8,128)(2,1)} %get-tuple-element.34.t_ref.refs_0_, bf16[128,4096]{1,0:T(8,128)(2,1)} %collective-permute-done.7.refs_1_, bf16[8192,1536]{1,0:T(8,128)(2,1)} %refs_2_.3, ...), custom_call_target="tpu_custom_call" | custom-call | flops 1 | bytes 1 | tf_op jit(solution)/shard_map/down3_0/pallas_call | solution.py:473
  151.5 2.4 %all-gather.7 = bf16[256,1536]{1,0:T(8,128)(2,1)S(1)} all-gather(bf16[128,1536]{1,0:T(8,128)(2,1)S(1)} %get-tuple-element.43), channel_id=9, replica_groups={{0,8},{16,24},{1,9},{17,25},{2,10},{18,26},{3,11},{19,27},{4,12},{20,28..., dimensions={0}, use_global_device_ids=true | all-gather | bytes 1179648 | tf_op jit(solution)/shard_map/all_gather | solution.py:353
  153.9 0.6 finish3.1
  154.5 4.1 %collective-permute-start.12 = (bf16[64,1536]{1,0:T(8,128)(2,1)S(1)}, bf16[64,1536]{1,0:T(8,128)(2,1)S(1)}, u32[]{:S(2)}, u32[]{:S(2)}) collective-permute-start(bf16[64,1536]{1,0:T(8,128)(2,1)S(1)} %get-tuple-element.46), channel_id=1, source_target_pairs={{0,5},{1,4},{2,7},{3,6},{4,1},{5,0},{6,3},{7,2},{8,13},{9,12},{10,... | collective-permute-start | bytes 589832 | tf_op jit(solution)/shard_map/ppermute | solution.py:507
  158.6 0.3 collective-permute-start.11
  159.0 0.0 all-to-all-done.2.refs_0_
  159.0 1.4 combine1.1.acc_ref.refs_2_
  160.4 0.0 collective-permute-done.10.refs_1_
  160.4 0.0 collective-permute-done.9.refs_0_
  160.4 1.4 combine2.1.acc_ref.refs_2_
  161.8 11.0 %collective-permute-done.12.refs_1_ = bf16[64,1536]{1,0:T(8,128)(2,1)S(1)} collective-permute-done((bf16[64,1536]{1,0:T(8,128)(2,1)S(1)}, bf16[64,1536]{1,0:T(8,128)(2,1)S(1)}, u32[]{:S(2)}, u32[]{:S(2)}) %collective-permute-start.12) | collective-permute-done | bytes 196640 | tf_op jit(solution)/shard_map/ppermute | solution.py:507
  172.8 3.8 %collective-permute-done.11.refs_0_ = bf16[64,1536]{1,0:T(8,128)(2,1)S(1)} collective-permute-done((bf16[64,1536]{1,0:T(8,128)(2,1)S(1)}, bf16[64,1536]{1,0:T(8,128)(2,1)S(1)}, u32[]{:S(2)}, u32[]{:S(2)}) %collective-permute-start.11) | collective-permute-done | bytes 196640 | tf_op jit(solution)/shard_map/ppermute | solution.py:507
  176.5 2.3 %combine3.1 = bf16[256,1536]{1,0:T(8,128)(2,1)} custom-call(s32[2]{0:T(128)S(1)} %copy-done.8, s32[2,256]{1,0:T(2,128)S(1)} %bitcast.25, f32[8,256]{1,0:T(8,128)S(1)} %copy-done.5, f32[8,256]{1,0:T(8,128)S(1)} %copy-done.3, f32[256,1536]{1,0:T(8,128)S(1)} %combine2.1.acc_ref.refs_2_, bf16[64,1536]{1,0:T(8,128)(2,1)S(1)} %collective-permute-done.11.refs_0_, ...), custom_call_target="tpu_custom_call" | custom-call | flops 1 | bytes 1 | tf_op jit(solution)/shard_map/combine3/pallas_call | solution.py:513
  (22 shorter events, 0.0 us)
Async XLA Ops:
  0.0 1.1 copy-start
  1.1 0.7 copy-start.9
  1.8 0.7 copy-start.11
  5.3 14.1 %copy-start.4 = (f32[8,256]{1,0:T(8,128)}, f32[8,256]{1,0:T(8,128)S(1)}, u32[]{:S(2)}) copy-start(f32[8,256]{1,0:T(8,128)S(1)} %get-tuple-element.26.t_ref.slot_ref) | copy-start | bytes 24580
  5.3 20.8 %all-to-all-start = ((bf16[4,64,1536]{2,1,0:T(8,128)(2,1)}), bf16[4,64,1536]{2,1,0:T(8,128)(2,1)S(1)}, u32[]{:S(2)}, u32[]{:S(2)}) async-start(bf16[4,64,1536]{2,1,0:T(8,128)(2,1)} %get-tuple-element.28), calls=%async_computation | async-start | bytes 1572864 | tf_op jit(solution)/shard_map/all_to_all | solution.py:356
  10.5 1.2 collective-permute-start
  11.7 14.4 %collective-permute-start.1 = (f32[8,256]{1,0:T(8,128)S(1)}, f32[8,256]{1,0:T(8,128)S(1)}, u32[]{:S(2)}, u32[]{:S(2)}) collective-permute-start(f32[8,256]{1,0:T(8,128)S(1)} %add.11), channel_id=1, source_target_pairs={{0,16},{8,24},{16,0},{24,8},{1,17},{9,25},{17,1},{25,9},{2,18},{10... | collective-permute-start | bytes 24584 | tf_op jit(solution)/shard_map/ppermute | solution.py:375
  13.3 6.2 %copy-start.6 = (s32[2]{0:T(128)}, s32[2]{0:T(128)S(1)}, u32[]{:S(2)}) copy-start(s32[2]{0:T(128)S(1)} %pad_add_fusion.me_ref) | copy-start | bytes 28
  19.3 22.1 %collective-permute-start.2 = (bf16[2048,1536]{1,0:T(8,128)(2,1)}, bf16[2048,1536]{1,0:T(8,128)(2,1)}, u32[]{:S(2)}, u32[]{:S(2)}) collective-permute-start(bf16[2048,1536]{1,0:T(8,128)(2,1)} %cut0.1.t_ref), channel_id=1, source_target_pairs={{0,8},{8,0},{16,24},{24,16},{1,9},{9,1},{17,25},{25,17},{2,10},{10... | collective-permute-start | bytes 18874376 | tf_op jit(solution)/shard_map/ppermute | solution.py:350
  25.5 33.2 %collective-permute-start.4 = (bf16[2048,1536]{1,0:T(8,128)(2,1)}, bf16[2048,1536]{1,0:T(8,128)(2,1)}, u32[]{:S(2)}, u32[]{:S(2)}) collective-permute-start(bf16[2048,1536]{1,0:T(8,128)(2,1)} %cut1.1.t_ref), channel_id=1, source_target_pairs={{0,8},{8,0},{16,24},{24,16},{1,9},{9,1},{17,25},{25,17},{2,10},{10... | collective-permute-start | bytes 18874376 | tf_op jit(solution)/shard_map/ppermute | solution.py:350
  26.1 54.9 %copy-start.2 = (f32[8,256]{1,0:T(8,128)}, f32[8,256]{1,0:T(8,128)S(1)}, u32[]{:S(2)}) copy-start(f32[8,256]{1,0:T(8,128)S(1)} %add.12.refs_8_.logit_ref) | copy-start | bytes 24580
  26.1 43.5 %all-to-all-start.1 = ((bf16[8,64,1536]{2,1,0:T(8,128)(2,1)}), bf16[8,64,1536]{2,1,0:T(8,128)(2,1)}, u32[]{:S(2)}, u32[]{:S(2)}) async-start(bf16[8,64,1536]{2,1,0:T(8,128)(2,1)} %get-tuple-element.31), calls=%async_computation.1 | async-start | bytes 3145728 | tf_op jit(solution)/shard_map/all_to_all | solution.py:371
  32.3 9.2 %copy-start.7 = (s32[2]{0:T(128)S(1)}, s32[2]{0:T(128)}, u32[]{:S(2)}) copy-start(s32[2]{0:T(128)} %copy-done.6) | copy-start | bytes 28
  48.0 46.9 %collective-permute-start.3 = (bf16[256,2048]{1,0:T(8,128)(2,1)S(1)}, bf16[256,2048]{1,0:T(8,128)(2,1)S(1)}, u32[]{:S(2)}, u32[]{:S(2)}) collective-permute-start(bf16[256,2048]{1,0:T(8,128)(2,1)S(1)} %up1_0.1.t_ref.a_ref), channel_id=1, source_target_pairs={{0,16},{8,24},{16,0},{24,8},{1,17},{9,25},{17,1},{25,9},{2,18},{10... | collective-permute-start | bytes 3145736 | tf_op jit(solution)/shard_map/ppermute | solution.py:456
  58.6 37.3 %collective-permute-start.6 = (bf16[4096,1536]{1,0:T(8,128)(2,1)}, bf16[4096,1536]{1,0:T(8,128)(2,1)}, u32[]{:S(2)}, u32[]{:S(2)}) collective-permute-start(bf16[4096,1536]{1,0:T(8,128)(2,1)} %cutNone.1.refs_7_), channel_id=1, source_target_pairs={{0,8},{8,0},{16,24},{24,16},{1,9},{9,1},{17,25},{25,17},{2,10},{10... | collective-permute-start | bytes 37748744 | tf_op jit(solution)/shard_map/ppermute | solution.py:350
  66.2 29.7 %collective-permute-start.5 = (bf16[256,2048]{1,0:T(8,128)(2,1)}, bf16[256,2048]{1,0:T(8,128)(2,1)}, u32[]{:S(2)}, u32[]{:S(2)}) collective-permute-start(bf16[256,2048]{1,0:T(8,128)(2,1)} %up1_2.1.t_ref.refs_1_), channel_id=1, source_target_pairs={{0,16},{8,24},{16,0},{24,8},{1,17},{9,25},{17,1},{25,9},{2,18},{10... | collective-permute-start | bytes 3145736 | tf_op jit(solution)/shard_map/ppermute | solution.py:456
  92.8 26.4 %collective-permute-start.8 = (bf16[128,4096]{1,0:T(8,128)(2,1)}, bf16[128,4096]{1,0:T(8,128)(2,1)}, u32[]{:S(2)}, u32[]{:S(2)}) collective-permute-start(bf16[128,4096]{1,0:T(8,128)(2,1)} %get-tuple-element.38.refs_0_), channel_id=1, source_target_pairs={{0,16},{8,24},{16,0},{24,8},{1,17},{9,25},{17,1},{25,9},{2,18},{10... | collective-permute-start | bytes 3145736 | tf_op jit(solution)/shard_map/ppermute | solution.py:456
  94.4 46.5 %collective-permute-start.7 = (bf16[128,4096]{1,0:T(8,128)(2,1)}, bf16[128,4096]{1,0:T(8,128)(2,1)}, u32[]{:S(2)}, u32[]{:S(2)}) collective-permute-start(bf16[128,4096]{1,0:T(8,128)(2,1)} %get-tuple-element.34.t_ref.refs_0_), channel_id=1, source_target_pairs={{0,16},{8,24},{16,0},{24,8},{1,17},{9,25},{17,1},{25,9},{2,18},{10... | collective-permute-start | bytes 3145736 | tf_op jit(solution)/shard_map/ppermute | solution.py:456
  113.7 45.3 %all-to-all-start.2 = ((bf16[4,64,1536]{2,1,0:T(8,128)(2,1)}), bf16[4,64,1536]{2,1,0:T(8,128)(2,1)S(1)}, u32[]{:S(2)}, u32[]{:S(2)}) async-start(bf16[4,64,1536]{2,1,0:T(8,128)(2,1)} %finish1.1.refs_4_), calls=%async_computation.2 | async-start | bytes 1572864 | tf_op jit(solution)/shard_map/all_to_all | solution.py:356
  117.9 23.0 %copy-start.8 = (s32[2]{0:T(128)S(1)}, s32[2]{0:T(128)}, u32[]{:S(2)}) copy-start(s32[2]{0:T(128)} %copy-done.6) | copy-start | bytes 28
  132.9 27.6 %collective-permute-start.10 = (bf16[64,1536]{1,0:T(8,128)(2,1)S(1)}, bf16[64,1536]{1,0:T(8,128)(2,1)S(1)}, u32[]{:S(2)}, u32[]{:S(2)}) collective-permute-start(bf16[64,1536]{1,0:T(8,128)(2,1)S(1)} %get-tuple-element.45), channel_id=1, source_target_pairs={{0,7},{1,6},{2,5},{3,4},{4,3},{5,2},{6,1},{7,0},{8,15},{9,14},{10,... | collective-permute-start | bytes 589832 | tf_op jit(solution)/shard_map/ppermute | solution.py:507
  137.9 21.1 %copy-start.1 = (bf16[256,1536]{1,0:T(8,128)(2,1)S(1)}, bf16[256,1536]{1,0:T(8,128)(2,1)}, u32[]{:S(2)}) copy-start(bf16[256,1536]{1,0:T(8,128)(2,1)} %acc_ref.1) | copy-start | bytes 2359300
  137.9 21.1 %copy-start.3 = (f32[8,256]{1,0:T(8,128)S(1)}, f32[8,256]{1,0:T(8,128)}, u32[]{:S(2)}) copy-start(f32[8,256]{1,0:T(8,128)} %copy-done.2) | copy-start | bytes 24580
  137.9 21.1 %copy-start.5 = (f32[8,256]{1,0:T(8,128)S(1)}, f32[8,256]{1,0:T(8,128)}, u32[]{:S(2)}) copy-start(f32[8,256]{1,0:T(8,128)} %copy-done.4) | copy-start | bytes 24580
  137.9 21.1 %copy-start.10 = (s32[256,2]{0,1:T(2,128)S(1)}, s32[256,2]{0,1:T(2,128)}, u32[]{:S(2)}) copy-start(s32[256,2]{0,1:T(2,128)} %param.9) | copy-start | bytes 6148
  137.9 22.6 %collective-permute-start.9 = (bf16[64,1536]{1,0:T(8,128)(2,1)S(1)}, bf16[64,1536]{1,0:T(8,128)(2,1)S(1)}, u32[]{:S(2)}, u32[]{:S(2)}) collective-permute-start(bf16[64,1536]{1,0:T(8,128)(2,1)S(1)} %get-tuple-element.41.refs_4_), channel_id=1, source_target_pairs={{0,6},{1,7},{2,4},{3,5},{4,2},{5,3},{6,0},{7,1},{8,14},{9,15},{10,... | collective-permute-start | bytes 589832 | tf_op jit(solution)/shard_map/ppermute | solution.py:507
  154.5 18.2 %collective-permute-start.12 = (bf16[64,1536]{1,0:T(8,128)(2,1)S(1)}, bf16[64,1536]{1,0:T(8,128)(2,1)S(1)}, u32[]{:S(2)}, u32[]{:S(2)}) collective-permute-start(bf16[64,1536]{1,0:T(8,128)(2,1)S(1)} %get-tuple-element.46), channel_id=1, source_target_pairs={{0,5},{1,4},{2,7},{3,6},{4,1},{5,0},{6,3},{7,2},{8,13},{9,12},{10,... | collective-permute-start | bytes 589832 | tf_op jit(solution)/shard_map/ppermute | solution.py:507
  158.6 17.9 %collective-permute-start.11 = (bf16[64,1536]{1,0:T(8,128)(2,1)S(1)}, bf16[64,1536]{1,0:T(8,128)(2,1)S(1)}, u32[]{:S(2)}, u32[]{:S(2)}) collective-permute-start(bf16[64,1536]{1,0:T(8,128)(2,1)S(1)} %get-tuple-element.44.refs_1_), channel_id=1, source_target_pairs={{0,4},{1,5},{2,6},{3,7},{4,0},{5,1},{6,2},{7,3},{8,12},{9,13},{10,... | collective-permute-start | bytes 589832 | tf_op jit(solution)/shard_map/ppermute | solution.py:507
